TPU v7x, 512 devices: a whole 4x4x16 slice. The times are simulated.
512 devices in a mesh: sec: 32 (over z_lo, x, core), tile: 16 (over y, z_hi).
Axes of the slice: x: 4, y: 4, z: 16 (z_hi: 4, z_lo: 4; z = z_hi * 4 + z_lo), core: 2. Of those that a mesh axis runs over, the one named last changes fastest.
Arguments:
- in_plane_force: float32 [2, 64, 1024, 256], P(None, 'sec', 'tile'), may hold values from -6 to 6
- stiffness: float32 [64, 1024, 256], P('sec', 'tile'), may hold values from 0.5 to 2
- stiffness_z: float32 [64, 1024, 256], P(None, ('tile', 'sec')), may hold values from 0.3 to 1.5
- patch_dest: int32 [32, 16, 256, 1], P('sec', 'tile'), may hold values from 0 to 31; in each aligned block of 256 rows (0 to 255, 256 to 511, ..., all dimensions but the last counted through in order) at most 16 rows name the same one
- patch_pos: int32 [32, 16, 256], P('sec', 'tile'), may hold values from 0 to 7
- patch_flow: float32 [32, 16, 256, 2, 128], P('sec', 'tile'), may hold values from -6 to 6
- patch_conf: float32 [32, 16, 256, 128], P('sec', 'tile'), may hold values from 0.2 to 1
Outputs:
- displacement: float32 [2, 64, 1024, 256], P(None, None, ('tile', 'sec'))
Inputs may be any that keep to these rules, and one draw needn't show every extreme that they name: `patch_dest`: among the 256 patches of one section group and tile, at most 16 name the same owner; in some of them an owner is named exactly 16 times.
All inputs are finite; a program needn't handle non-finite values.
Results may differ from a plain program's by a relative error of at most 0.00002.
Values sent between devices are 32-bit elements; how exact they have to be, the bound alone decides.
A program may use at most 64 MiB of HBM per device.

v0:
```python
import jax
import jax.numpy as jnp
from jax import lax
from jax.sharding import PartitionSpec as P

ISTEPS = 8
ZSTEPS = 8


STEP_PLANE = 0.12
STEP_CROSS = 0.15


def padded(shard, sides, width):
    for axis, dim in sides:
        count, length = (lax.axis_size(axis), shard.shape[dim])
        up = [(i, (i + 1) % count) for i in range(count - 1)]
        down = [(j, i) for i, j in up]
        last = lax.slice_in_dim(shard, length - width, length, axis=dim)
        leading = lax.slice_in_dim(shard, 0, width, axis=dim)
        before = lax.ppermute(last, axis, up)
        after = lax.ppermute(leading, axis, down)
        shard = jnp.concatenate([before, shard, after], axis=dim)
    return shard


def plane_step(extended, force, stiff):
    centre = extended[:, :, 1:-1]
    zero_column = jnp.zeros(centre.shape[:-1] + (1,), jnp.float32)
    left = jnp.concatenate([zero_column, centre[..., :-1]], axis=-1)
    right = jnp.concatenate([centre[..., 1:], zero_column], axis=-1)
    laplace = extended[:, :, 2:] + extended[:, :, :-2] + right + left - 4.0 * centre
    return centre + STEP_PLANE * (stiff * laplace + force)


def cross_steps(field, pull, weight, stiffness_z):
    for step in range(ZSTEPS):
        zero_layer = jnp.zeros(field.shape[:1] + (1,) + field.shape[2:], jnp.float32)
        below = jnp.concatenate([zero_layer, field[:, :-1]], axis=1)
        above = jnp.concatenate([field[:, 1:], zero_layer], axis=1)
        stretch = pull - weight[None] * (field - below)
        stretch_above = jnp.concatenate([stretch[:, 1:], zero_layer], axis=1)
        field = field + STEP_CROSS * (
            stiffness_z[None] * (above + below - 2.0 * field) + stretch - stretch_above
        )
    return field


def spread(target, payload, layers, rows, blocks):
    width = payload.shape[2]
    grid = jnp.zeros((layers * rows * blocks, 3, width), jnp.float32).at[target].add(payload)
    grid = grid.reshape(layers, rows, blocks, 3, width).transpose(3, 0, 1, 2, 4)
    return grid.reshape(3, layers, rows, blocks * width)


def per_device(
    in_plane_force, stiffness, stiffness_z, patch_dest, patch_pos, patch_flow, patch_conf
):
    groups = lax.axis_size("sec")
    layers, rows, columns = stiffness.shape
    inner_rows = rows // groups
    width = patch_flow.shape[-1]
    blocks = columns // width
    count = patch_pos.shape[2]
    field = STEP_PLANE * in_plane_force
    for step in range(1, ISTEPS):
        extended = padded(field, (("tile", 2),), 1)
        field = plane_step(extended, in_plane_force, stiffness[None])
    owner = patch_dest.reshape(count)
    place = patch_pos.reshape(count)
    layer = place // (inner_rows * blocks)
    inner_row = place // blocks % inner_rows
    column_block = place % blocks
    confidence = patch_conf.reshape(count, width)
    flow = patch_flow.reshape(count, 2, width)
    payload = jnp.concatenate([confidence[:, None, :] * flow, confidence[:, None, :]], axis=1)
    capacity = 2 * count // groups
    owners = jnp.arange(groups, dtype=jnp.int32)
    member = (owner[:, None] == owners[None, :]).astype(jnp.int32)
    earlier = jnp.cumsum(member, axis=0) - member
    slot = jnp.sum(earlier * member, axis=1)
    section = lax.axis_index("sec") * layers + layer
    target = (section * inner_rows + inner_row) * blocks + column_block
    outgoing = jnp.zeros((groups, capacity, 3, width), jnp.float32).at[owner, slot].set(payload)
    out_target = jnp.zeros((groups, capacity), jnp.int32).at[owner, slot].set(target)
    received, received_target = (
        lax.all_to_all(outgoing, "sec", split_axis=0, concat_axis=0, tiled=True),
        lax.all_to_all(out_target, "sec", split_axis=0, concat_axis=0, tiled=True),
    )
    moved = lax.all_to_all(field, "sec", split_axis=2, concat_axis=1, tiled=True)
    forces = spread(
        received_target.reshape(-1),
        received.reshape(-1, 3, width),
        layers * groups,
        inner_rows,
        blocks,
    )
    return cross_steps(moved, forces[:2], forces[2], stiffness_z)


def solution(mesh):
    placed = (
        P(None, "sec", "tile", None),
        P("sec", "tile", None),
        P(None, ("tile", "sec"), None),
        P("sec", "tile", None, None),
        P("sec", "tile", None),
        P("sec", "tile", None, None, None),
        P("sec", "tile", None, None),
    )
    return jax.shard_map(
        per_device,
        mesh=mesh,
        in_specs=placed,
        out_specs=P(None, None, ("tile", "sec"), None),
        check_vma=False,
    )
```

profile of v0, /device:TPU:25, one launch (start us, length us, event | category | flops | bytes accessed | tf_op | source)
XLA Modules:
  0.0 212.3 jit_solution(3188162330934515225)
XLA Ops:
  0.0 1.2 broadcast_multiply_fusion
  1.2 12.6 %collective-permute-start = (f32[2,2,1,256]{3,1,0,2:T(2,128)S(1)}, f32[2,2,1,256]{3,1,0,2:T(2,128)S(1)}, u32[]{:S(2)}, u32[]{:S(2)}) collective-permute-start(f32[2,2,1,256]{3,1,0,2:T(2,128)S(1)} %get-tuple-element.47), channel_id=1, source_target_pairs={{1,0},{2,1},{3,2},{4,3},{5,4},{6,5},{7,6},{8,7},{9,8},{10,9},{11,1... | collective-permute-start | bytes 12296 | tf_op jit(solution)/shard_map/ppermute | solution.py:22
  13.9 1.9 collective-permute-start.1
  15.8 0.7 copy-done.5
  16.5 0.6 reduce-window.6
  17.4 0.7 copy-done.6
  18.1 12.7 %scatter_fusion = s32[32,16]{0,1:T(8,128)S(1)} fusion(s32[32,16]{0,1:T(8,128)S(1)} %broadcast_in_dim.7, s32[256]{0:T(256)S(1)} %bitcast.43, s32[256]{0:T(256)S(1)} %fusion.34), kind=kCustom, calls=%fused_computation | custom fusion | bytes 5120 | tf_op jit(solution)/shard_map/scatter | solution.py:85
  30.9 0.7 copy.121
  31.6 6.8 %all-to-all-start.1 = ((s32[32,1,16]{2,1,0:T(1,128)}), s32[32,1,16]{2,1,0:T(1,128)S(1)}, u32[]{:S(2)}, u32[]{:S(2)}) async-start(s32[32,1,16]{2,1,0:T(1,128)} %copy.121), calls=%async_computation.1 | async-start | bytes 32768 | tf_op jit(solution)/shard_map/all_to_all | solution.py:88
  38.7 0.6 copy-done.4
  39.4 0.8 copy-done
  40.2 0.6 multiply_add_fusion.14
  40.8 8.4 %collective-permute-start.2 = (f32[2,2,1,256]{3,1,0,2:T(2,128)S(1)}, f32[2,2,1,256]{3,1,0,2:T(2,128)S(1)}, u32[]{:S(2)}, u32[]{:S(2)}) collective-permute-start(f32[2,2,1,256]{3,1,0,2:T(2,128)S(1)} %get-tuple-element.43), channel_id=1, source_target_pairs={{1,0},{2,1},{3,2},{4,3},{5,4},{6,5},{7,6},{8,7},{9,8},{10,9},{11,1... | collective-permute-start | bytes 12296 | tf_op jit(solution)/shard_map/ppermute | solution.py:22
  49.3 1.9 collective-permute-start.3
  51.6 6.9 %collective-permute-done.3 = f32[2,2,1,256]{3,1,0,2:T(2,128)S(1)} collective-permute-done((f32[2,2,1,256]{3,1,0,2:T(2,128)S(1)}, f32[2,2,1,256]{3,1,0,2:T(2,128)S(1)}, u32[]{:S(2)}, u32[]{:S(2)}) %collective-permute-start.3) | collective-permute-done | bytes 4128 | tf_op jit(solution)/shard_map/ppermute | solution.py:21
  58.5 0.6 multiply_add_fusion.13
  59.1 3.4 %collective-permute-start.4 = (f32[2,2,1,256]{3,1,0,2:T(2,128)S(1)}, f32[2,2,1,256]{3,1,0,2:T(2,128)S(1)}, u32[]{:S(2)}, u32[]{:S(2)}) collective-permute-start(f32[2,2,1,256]{3,1,0,2:T(2,128)S(1)} %get-tuple-element.39), channel_id=1, source_target_pairs={{1,0},{2,1},{3,2},{4,3},{5,4},{6,5},{7,6},{8,7},{9,8},{10,9},{11,1... | collective-permute-start | bytes 12296 | tf_op jit(solution)/shard_map/ppermute | solution.py:22
  62.4 5.8 %collective-permute-start.5 = (f32[2,2,1,256]{3,1,0,2:T(2,128)S(1)}, f32[2,2,1,256]{3,1,0,2:T(2,128)S(1)}, u32[]{:S(2)}, u32[]{:S(2)}) collective-permute-start(f32[2,2,1,256]{3,1,0,2:T(2,128)S(1)} %get-tuple-element.40), channel_id=1, source_target_pairs={{0,1},{1,2},{2,3},{3,4},{4,5},{5,6},{6,7},{7,8},{8,9},{9,10},{10,1... | collective-permute-start | bytes 12296 | tf_op jit(solution)/shard_map/ppermute | solution.py:21
  68.6 3.0 %collective-permute-done.5 = f32[2,2,1,256]{3,1,0,2:T(2,128)S(1)} collective-permute-done((f32[2,2,1,256]{3,1,0,2:T(2,128)S(1)}, f32[2,2,1,256]{3,1,0,2:T(2,128)S(1)}, u32[]{:S(2)}, u32[]{:S(2)}) %collective-permute-start.5) | collective-permute-done | bytes 4128 | tf_op jit(solution)/shard_map/ppermute | solution.py:21
  71.6 0.6 multiply_add_fusion.12
  72.2 2.4 %collective-permute-start.6 = (f32[2,2,1,256]{3,1,0,2:T(2,128)S(1)}, f32[2,2,1,256]{3,1,0,2:T(2,128)S(1)}, u32[]{:S(2)}, u32[]{:S(2)}) collective-permute-start(f32[2,2,1,256]{3,1,0,2:T(2,128)S(1)} %get-tuple-element.35), channel_id=1, source_target_pairs={{1,0},{2,1},{3,2},{4,3},{5,4},{6,5},{7,6},{8,7},{9,8},{10,9},{11,1... | collective-permute-start | bytes 12296 | tf_op jit(solution)/shard_map/ppermute | solution.py:22
  74.6 6.8 %collective-permute-start.7 = (f32[2,2,1,256]{3,1,0,2:T(2,128)S(1)}, f32[2,2,1,256]{3,1,0,2:T(2,128)S(1)}, u32[]{:S(2)}, u32[]{:S(2)}) collective-permute-start(f32[2,2,1,256]{3,1,0,2:T(2,128)S(1)} %get-tuple-element.36), channel_id=1, source_target_pairs={{0,1},{1,2},{2,3},{3,4},{4,5},{5,6},{6,7},{7,8},{8,9},{9,10},{10,1... | collective-permute-start | bytes 12296 | tf_op jit(solution)/shard_map/ppermute | solution.py:21
  81.8 2.0 collective-permute-done.7
  83.8 0.6 multiply_add_fusion.11
  84.4 3.6 %collective-permute-start.8 = (f32[2,2,1,256]{3,1,0,2:T(2,128)S(1)}, f32[2,2,1,256]{3,1,0,2:T(2,128)S(1)}, u32[]{:S(2)}, u32[]{:S(2)}) collective-permute-start(f32[2,2,1,256]{3,1,0,2:T(2,128)S(1)} %get-tuple-element.31), channel_id=1, source_target_pairs={{1,0},{2,1},{3,2},{4,3},{5,4},{6,5},{7,6},{8,7},{9,8},{10,9},{11,1... | collective-permute-start | bytes 12296 | tf_op jit(solution)/shard_map/ppermute | solution.py:22
  88.0 5.6 %collective-permute-start.9 = (f32[2,2,1,256]{3,1,0,2:T(2,128)S(1)}, f32[2,2,1,256]{3,1,0,2:T(2,128)S(1)}, u32[]{:S(2)}, u32[]{:S(2)}) collective-permute-start(f32[2,2,1,256]{3,1,0,2:T(2,128)S(1)} %get-tuple-element.32), channel_id=1, source_target_pairs={{0,1},{1,2},{2,3},{3,4},{4,5},{5,6},{6,7},{7,8},{8,9},{9,10},{10,1... | collective-permute-start | bytes 12296 | tf_op jit(solution)/shard_map/ppermute | solution.py:21
  94.0 3.2 %collective-permute-done.9 = f32[2,2,1,256]{3,1,0,2:T(2,128)S(1)} collective-permute-done((f32[2,2,1,256]{3,1,0,2:T(2,128)S(1)}, f32[2,2,1,256]{3,1,0,2:T(2,128)S(1)}, u32[]{:S(2)}, u32[]{:S(2)}) %collective-permute-start.9) | collective-permute-done | bytes 4128 | tf_op jit(solution)/shard_map/ppermute | solution.py:21
  97.2 0.6 multiply_add_fusion.10
  97.8 6.2 %collective-permute-start.10 = (f32[2,2,1,256]{3,1,0,2:T(2,128)S(1)}, f32[2,2,1,256]{3,1,0,2:T(2,128)S(1)}, u32[]{:S(2)}, u32[]{:S(2)}) collective-permute-start(f32[2,2,1,256]{3,1,0,2:T(2,128)S(1)} %get-tuple-element.27), channel_id=1, source_target_pairs={{1,0},{2,1},{3,2},{4,3},{5,4},{6,5},{7,6},{8,7},{9,8},{10,9},{11,1... | collective-permute-start | bytes 12296 | tf_op jit(solution)/shard_map/ppermute | solution.py:22
  104.0 3.0 %collective-permute-start.11 = (f32[2,2,1,256]{3,1,0,2:T(2,128)S(1)}, f32[2,2,1,256]{3,1,0,2:T(2,128)S(1)}, u32[]{:S(2)}, u32[]{:S(2)}) collective-permute-start(f32[2,2,1,256]{3,1,0,2:T(2,128)S(1)} %get-tuple-element.28), channel_id=1, source_target_pairs={{0,1},{1,2},{2,3},{3,4},{4,5},{5,6},{6,7},{7,8},{8,9},{9,10},{10,1... | collective-permute-start | bytes 12296 | tf_op jit(solution)/shard_map/ppermute | solution.py:21
  107.3 5.8 %collective-permute-done.11 = f32[2,2,1,256]{3,1,0,2:T(2,128)S(1)} collective-permute-done((f32[2,2,1,256]{3,1,0,2:T(2,128)S(1)}, f32[2,2,1,256]{3,1,0,2:T(2,128)S(1)}, u32[]{:S(2)}, u32[]{:S(2)}) %collective-permute-start.11) | collective-permute-done | bytes 4128 | tf_op jit(solution)/shard_map/ppermute | solution.py:21
  113.1 0.6 multiply_add_fusion.9
  113.7 3.4 %collective-permute-start.12 = (f32[2,2,1,256]{3,1,0,2:T(2,128)S(1)}, f32[2,2,1,256]{3,1,0,2:T(2,128)S(1)}, u32[]{:S(2)}, u32[]{:S(2)}) collective-permute-start(f32[2,2,1,256]{3,1,0,2:T(2,128)S(1)} %get-tuple-element.23), channel_id=1, source_target_pairs={{1,0},{2,1},{3,2},{4,3},{5,4},{6,5},{7,6},{8,7},{9,8},{10,9},{11,1... | collective-permute-start | bytes 12296 | tf_op jit(solution)/shard_map/ppermute | solution.py:22
  117.1 5.8 %collective-permute-start.13 = (f32[2,2,1,256]{3,1,0,2:T(2,128)S(1)}, f32[2,2,1,256]{3,1,0,2:T(2,128)S(1)}, u32[]{:S(2)}, u32[]{:S(2)}) collective-permute-start(f32[2,2,1,256]{3,1,0,2:T(2,128)S(1)} %get-tuple-element.24), channel_id=1, source_target_pairs={{0,1},{1,2},{2,3},{3,4},{4,5},{5,6},{6,7},{7,8},{8,9},{9,10},{10,1... | collective-permute-start | bytes 12296 | tf_op jit(solution)/shard_map/ppermute | solution.py:21
  123.3 3.0 %collective-permute-done.13 = f32[2,2,1,256]{3,1,0,2:T(2,128)S(1)} collective-permute-done((f32[2,2,1,256]{3,1,0,2:T(2,128)S(1)}, f32[2,2,1,256]{3,1,0,2:T(2,128)S(1)}, u32[]{:S(2)}, u32[]{:S(2)}) %collective-permute-start.13) | collective-permute-done | bytes 4128 | tf_op jit(solution)/shard_map/ppermute | solution.py:21
  126.3 1.3 multiply_add_fusion.8
  127.6 16.5 %all-to-all-start = ((f32[2,2,64,256]{3,1,0,2:T(2,128)}), f32[2,2,64,256]{3,1,0,2:T(2,128)S(1)}, u32[]{:S(2)}, u32[]{:S(2)}) async-start(f32[2,2,64,256]{3,1,0,2:T(2,128)} %multiply_add_fusion.8), calls=%async_computation | async-start | bytes 524288 | tf_op jit(solution)/shard_map/all_to_all | solution.py:90
  144.8 9.8 %scatter_fusion.1 = f32[32,16,3,128]{3,2,1,0:T(4,128)S(1)} fusion(f32[32,16,3,128]{3,2,1,0:T(4,128)S(1)} %broadcast_in_dim.8, s32[256]{0:T(256)S(1)} %bitcast.44, f32[256,3,128]{2,1,0:T(4,128)S(1)} %pad_maximum_fusion), kind=kCustom, calls=%fused_computation.1 | custom fusion | bytes 1181696 | tf_op jit(solution)/shard_map/scatter | solution.py:84
  154.6 1.0 copy.123
  155.5 7.7 %all-to-all-start.2 = ((f32[32,16,3,128]{3,1,2,0:T(8,128)}), f32[32,16,3,128]{3,1,2,0:T(8,128)S(1)}, u32[]{:S(2)}, u32[]{:S(2)}) async-start(f32[32,16,3,128]{3,1,2,0:T(8,128)} %copy.123), calls=%async_computation.2 | async-start | bytes 1572864 | tf_op jit(solution)/shard_map/all_to_all | solution.py:87
  163.3 0.5 broadcast.267
  163.8 0.7 reduce.9
  164.9 20.0 %all-to-all-done.2 = f32[32,16,3,128]{3,1,2,0:T(8,128)S(1)} async-done(((f32[32,16,3,128]{3,1,2,0:T(8,128)}), f32[32,16,3,128]{3,1,2,0:T(8,128)S(1)}, u32[]{:S(2)}, u32[]{:S(2)}) %all-to-all-start.2) | async-done | bytes 786464 | tf_op jit(solution)/shard_map/all_to_all | solution.py:87
  184.9 0.5 copy.125
  185.6 17.8 %scatter_fusion.2 = f32[256,3,128]{2,1,0:T(4,128)S(1)} fusion(f32[256,3,128]{2,1,0:T(4,128)S(1)} %broadcast_in_dim.6, s32[512]{0:T(512)S(1)} %bitcast.56, f32[512,3,128]{2,1,0:T(4,128)S(1)} %copy.125), kind=kCustom, calls=%fused_computation.2 | custom fusion | flops 196608 | bytes 2361344 | tf_op jit(solution)/shard_map/scatter-add | solution.py:51
  203.5 0.4 slice_reduce_fusion
  204.8 0.9 copy-done.1
  211.2 1.1 multiply_add_fusion
  (85 shorter events, 10.2 us)
Async XLA Ops:
  1.2 38.1 %collective-permute-start = (f32[2,2,1,256]{3,1,0,2:T(2,128)S(1)}, f32[2,2,1,256]{3,1,0,2:T(2,128)S(1)}, u32[]{:S(2)}, u32[]{:S(2)}) collective-permute-start(f32[2,2,1,256]{3,1,0,2:T(2,128)S(1)} %get-tuple-element.47), channel_id=1, source_target_pairs={{1,0},{2,1},{3,2},{4,3},{5,4},{6,5},{7,6},{8,7},{9,8},{10,9},{11,1... | collective-permute-start | bytes 12296 | tf_op jit(solution)/shard_map/ppermute | solution.py:22
  13.9 25.5 %collective-permute-start.1 = (f32[2,2,1,256]{3,1,0,2:T(2,128)S(1)}, f32[2,2,1,256]{3,1,0,2:T(2,128)S(1)}, u32[]{:S(2)}, u32[]{:S(2)}) collective-permute-start(f32[2,2,1,256]{3,1,0,2:T(2,128)S(1)} %get-tuple-element.48), channel_id=1, source_target_pairs={{0,1},{1,2},{2,3},{3,4},{4,5},{5,6},{6,7},{7,8},{8,9},{9,10},{10,1... | collective-permute-start | bytes 12296 | tf_op jit(solution)/shard_map/ppermute | solution.py:21
  15.8 0.7 copy-start.5
  17.4 0.7 copy-start.6
  31.6 96.0 %all-to-all-start.1 = ((s32[32,1,16]{2,1,0:T(1,128)}), s32[32,1,16]{2,1,0:T(1,128)S(1)}, u32[]{:S(2)}, u32[]{:S(2)}) async-start(s32[32,1,16]{2,1,0:T(1,128)} %copy.121), calls=%async_computation.1 | async-start | bytes 32768 | tf_op jit(solution)/shard_map/all_to_all | solution.py:88
  38.4 0.9 copy-start.4
  39.3 0.9 copy-start
  40.8 10.7 %collective-permute-start.2 = (f32[2,2,1,256]{3,1,0,2:T(2,128)S(1)}, f32[2,2,1,256]{3,1,0,2:T(2,128)S(1)}, u32[]{:S(2)}, u32[]{:S(2)}) collective-permute-start(f32[2,2,1,256]{3,1,0,2:T(2,128)S(1)} %get-tuple-element.43), channel_id=1, source_target_pairs={{1,0},{2,1},{3,2},{4,3},{5,4},{6,5},{7,6},{8,7},{9,8},{10,9},{11,1... | collective-permute-start | bytes 12296 | tf_op jit(solution)/shard_map/ppermute | solution.py:22
  49.3 9.2 %collective-permute-start.3 = (f32[2,2,1,256]{3,1,0,2:T(2,128)S(1)}, f32[2,2,1,256]{3,1,0,2:T(2,128)S(1)}, u32[]{:S(2)}, u32[]{:S(2)}) collective-permute-start(f32[2,2,1,256]{3,1,0,2:T(2,128)S(1)} %get-tuple-element.44), channel_id=1, source_target_pairs={{0,1},{1,2},{2,3},{3,4},{4,5},{5,6},{6,7},{7,8},{8,9},{9,10},{10,1... | collective-permute-start | bytes 12296 | tf_op jit(solution)/shard_map/ppermute | solution.py:21
  59.1 9.5 %collective-permute-start.4 = (f32[2,2,1,256]{3,1,0,2:T(2,128)S(1)}, f32[2,2,1,256]{3,1,0,2:T(2,128)S(1)}, u32[]{:S(2)}, u32[]{:S(2)}) collective-permute-start(f32[2,2,1,256]{3,1,0,2:T(2,128)S(1)} %get-tuple-element.39), channel_id=1, source_target_pairs={{1,0},{2,1},{3,2},{4,3},{5,4},{6,5},{7,6},{8,7},{9,8},{10,9},{11,1... | collective-permute-start | bytes 12296 | tf_op jit(solution)/shard_map/ppermute | solution.py:22
  62.4 9.2 %collective-permute-start.5 = (f32[2,2,1,256]{3,1,0,2:T(2,128)S(1)}, f32[2,2,1,256]{3,1,0,2:T(2,128)S(1)}, u32[]{:S(2)}, u32[]{:S(2)}) collective-permute-start(f32[2,2,1,256]{3,1,0,2:T(2,128)S(1)} %get-tuple-element.40), channel_id=1, source_target_pairs={{0,1},{1,2},{2,3},{3,4},{4,5},{5,6},{6,7},{7,8},{8,9},{9,10},{10,1... | collective-permute-start | bytes 12296 | tf_op jit(solution)/shard_map/ppermute | solution.py:21
  72.2 9.5 %collective-permute-start.6 = (f32[2,2,1,256]{3,1,0,2:T(2,128)S(1)}, f32[2,2,1,256]{3,1,0,2:T(2,128)S(1)}, u32[]{:S(2)}, u32[]{:S(2)}) collective-permute-start(f32[2,2,1,256]{3,1,0,2:T(2,128)S(1)} %get-tuple-element.35), channel_id=1, source_target_pairs={{1,0},{2,1},{3,2},{4,3},{5,4},{6,5},{7,6},{8,7},{9,8},{10,9},{11,1... | collective-permute-start | bytes 12296 | tf_op jit(solution)/shard_map/ppermute | solution.py:22
  74.6 9.2 %collective-permute-start.7 = (f32[2,2,1,256]{3,1,0,2:T(2,128)S(1)}, f32[2,2,1,256]{3,1,0,2:T(2,128)S(1)}, u32[]{:S(2)}, u32[]{:S(2)}) collective-permute-start(f32[2,2,1,256]{3,1,0,2:T(2,128)S(1)} %get-tuple-element.36), channel_id=1, source_target_pairs={{0,1},{1,2},{2,3},{3,4},{4,5},{5,6},{6,7},{7,8},{8,9},{9,10},{10,1... | collective-permute-start | bytes 12296 | tf_op jit(solution)/shard_map/ppermute | solution.py:21
  84.4 9.5 %collective-permute-start.8 = (f32[2,2,1,256]{3,1,0,2:T(2,128)S(1)}, f32[2,2,1,256]{3,1,0,2:T(2,128)S(1)}, u32[]{:S(2)}, u32[]{:S(2)}) collective-permute-start(f32[2,2,1,256]{3,1,0,2:T(2,128)S(1)} %get-tuple-element.31), channel_id=1, source_target_pairs={{1,0},{2,1},{3,2},{4,3},{5,4},{6,5},{7,6},{8,7},{9,8},{10,9},{11,1... | collective-permute-start | bytes 12296 | tf_op jit(solution)/shard_map/ppermute | solution.py:22
  88.0 9.2 %collective-permute-start.9 = (f32[2,2,1,256]{3,1,0,2:T(2,128)S(1)}, f32[2,2,1,256]{3,1,0,2:T(2,128)S(1)}, u32[]{:S(2)}, u32[]{:S(2)}) collective-permute-start(f32[2,2,1,256]{3,1,0,2:T(2,128)S(1)} %get-tuple-element.32), channel_id=1, source_target_pairs={{0,1},{1,2},{2,3},{3,4},{4,5},{5,6},{6,7},{7,8},{8,9},{9,10},{10,1... | collective-permute-start | bytes 12296 | tf_op jit(solution)/shard_map/ppermute | solution.py:21
  97.8 9.5 %collective-permute-start.10 = (f32[2,2,1,256]{3,1,0,2:T(2,128)S(1)}, f32[2,2,1,256]{3,1,0,2:T(2,128)S(1)}, u32[]{:S(2)}, u32[]{:S(2)}) collective-permute-start(f32[2,2,1,256]{3,1,0,2:T(2,128)S(1)} %get-tuple-element.27), channel_id=1, source_target_pairs={{1,0},{2,1},{3,2},{4,3},{5,4},{6,5},{7,6},{8,7},{9,8},{10,9},{11,1... | collective-permute-start | bytes 12296 | tf_op jit(solution)/shard_map/ppermute | solution.py:22
  104.0 9.2 %collective-permute-start.11 = (f32[2,2,1,256]{3,1,0,2:T(2,128)S(1)}, f32[2,2,1,256]{3,1,0,2:T(2,128)S(1)}, u32[]{:S(2)}, u32[]{:S(2)}) collective-permute-start(f32[2,2,1,256]{3,1,0,2:T(2,128)S(1)} %get-tuple-element.28), channel_id=1, source_target_pairs={{0,1},{1,2},{2,3},{3,4},{4,5},{5,6},{6,7},{7,8},{8,9},{9,10},{10,1... | collective-permute-start | bytes 12296 | tf_op jit(solution)/shard_map/ppermute | solution.py:21
  113.7 9.5 %collective-permute-start.12 = (f32[2,2,1,256]{3,1,0,2:T(2,128)S(1)}, f32[2,2,1,256]{3,1,0,2:T(2,128)S(1)}, u32[]{:S(2)}, u32[]{:S(2)}) collective-permute-start(f32[2,2,1,256]{3,1,0,2:T(2,128)S(1)} %get-tuple-element.23), channel_id=1, source_target_pairs={{1,0},{2,1},{3,2},{4,3},{5,4},{6,5},{7,6},{8,7},{9,8},{10,9},{11,1... | collective-permute-start | bytes 12296 | tf_op jit(solution)/shard_map/ppermute | solution.py:22
  117.1 9.2 %collective-permute-start.13 = (f32[2,2,1,256]{3,1,0,2:T(2,128)S(1)}, f32[2,2,1,256]{3,1,0,2:T(2,128)S(1)}, u32[]{:S(2)}, u32[]{:S(2)}) collective-permute-start(f32[2,2,1,256]{3,1,0,2:T(2,128)S(1)} %get-tuple-element.24), channel_id=1, source_target_pairs={{0,1},{1,2},{2,3},{3,4},{4,5},{5,6},{6,7},{7,8},{8,9},{9,10},{10,1... | collective-permute-start | bytes 12296 | tf_op jit(solution)/shard_map/ppermute | solution.py:21
  127.6 16.6 %copy-start.2 = (f32[1,1,256,128]{3,2,1,0:T(8,128)S(1)}, f32[1,1,256,128]{3,2,1,0:T(8,128)}, u32[]{:S(2)}) copy-start(f32[1,1,256,128]{3,2,1,0:T(8,128)} %param.13) | copy-start | bytes 393220
  127.6 16.6 %copy-start.3 = (f32[1,1,256,2,128]{4,3,2,1,0:T(2,128)S(1)}, f32[1,1,256,2,128]{4,3,2,1,0:T(2,128)}, u32[]{:S(2)}) copy-start(f32[1,1,256,2,128]{4,3,2,1,0:T(2,128)} %param.12) | copy-start | bytes 786436
  127.6 27.9 %all-to-all-start = ((f32[2,2,64,256]{3,1,0,2:T(2,128)}), f32[2,2,64,256]{3,1,0,2:T(2,128)S(1)}, u32[]{:S(2)}, u32[]{:S(2)}) async-start(f32[2,2,64,256]{3,1,0,2:T(2,128)} %multiply_add_fusion.8), calls=%async_computation | async-start | bytes 524288 | tf_op jit(solution)/shard_map/all_to_all | solution.py:90
  155.5 29.3 %all-to-all-start.2 = ((f32[32,16,3,128]{3,1,2,0:T(8,128)}), f32[32,16,3,128]{3,1,2,0:T(8,128)S(1)}, u32[]{:S(2)}, u32[]{:S(2)}) async-start(f32[32,16,3,128]{3,1,2,0:T(8,128)} %copy.123), calls=%async_computation.2 | async-start | bytes 1572864 | tf_op jit(solution)/shard_map/all_to_all | solution.py:87
  204.8 0.9 copy-start.1
where the time goes:
time: 213 us; the launch traced here: 212 us
  starting transfers between devices  102 us (48%)
  waiting for transfers between devices  44 us (21%)
  local copies, waits for them, and re-layouts  34.4 us (16%)
  other arithmetic  31.3 us (15%)
    ppermute x7, starting transfers between devices, padded(): after = lax.ppermute(leading, axis, down)  40 us
    ppermute x7, starting transfers between devices, padded(): before = lax.ppermute(last, axis, up)  30.8 us
    ppermute x7, waiting for transfers between devices, padded(): before = lax.ppermute(last, axis, up)  23.9 us
    all_to_all x1, waiting for transfers between devices, per_device(): lax.all_to_all(outgoing, 'sec', split_axis=0, concat_axis=0, tiled=True)  20 us
    scatter-add x1, other arithmetic, spread(): jnp.zeros((layers * rows * blocks, 3, width), jnp.float32).at[target]  17.8 us
    all_to_all x1, starting transfers between devices, per_device(): lax.all_to_all(field, 'sec', split_axis=2, concat_axis=1, tiled=True)  16.5 us
    scatter x1, local copies, waits for them, and re-layouts, per_device(): jnp.zeros((groups, capacity), jnp.int32).at[owner, slot].set(target)  12.7 us
    scatter x2, local copies, waits for them, and re-layouts, per_device(): jnp.zeros((groups, capacity, 3, width), jnp.float32).at[owner, slot]  10.7 us
  transfers between devices with their start and end apart: 17, of which 7 were waited for; matrix products, arithmetic and copies ran while one was open for 16% of the time, Pallas kernels for 0%

commit v1 on v0

v1 whole, which is shorter than its diff:
```python
import functools

import jax
import jax.numpy as jnp
from jax import lax
from jax.experimental import pallas as pl
from jax.experimental.pallas import tpu as pltpu
from jax.sharding import PartitionSpec as P

ISTEPS = 8
ZSTEPS = 8
STEP_PLANE = 0.12
STEP_CROSS = 0.15
LANES = 128
HALO = 8


def plane_steps(force, stiff):
    column = lax.broadcasted_iota(jnp.int32, force.shape, 2)
    first, last = column == 0, column == force.shape[2] - 1
    field = STEP_PLANE * force
    for _ in range(1, ISTEPS):
        up = pltpu.roll(field, 1, 1)
        down = pltpu.roll(field, field.shape[1] - 1, 1)
        left = jnp.where(first, 0.0, pltpu.roll(field, 1, 2))
        right = jnp.where(last, 0.0, pltpu.roll(field, field.shape[2] - 1, 2))
        laplace = (up + down) + (left + right) - 4.0 * field
        field = field + STEP_PLANE * (stiff * laplace + force)
    return field


def split3(value):
    high = value.astype(jnp.bfloat16)
    rest = value - high.astype(jnp.float32)
    middle = rest.astype(jnp.bfloat16)
    low = (rest - middle.astype(jnp.float32)).astype(jnp.bfloat16)
    return high, middle, low


def pair_halves(a, b):
    lower = lax.broadcasted_iota(jnp.int32, a.shape, 1) < 4
    return jnp.where(lower, a, pltpu.roll(b, 4, 1)), jnp.where(lower, pltpu.roll(a, 4, 1), b)


def body(
    force_hbm, stiff_hbm, cross_hbm, dest_hbm, pos_hbm, flow_hbm, conf_hbm, out_ref,
    fbuf, sbuf, zbuf, dest, pos, flow, conf, vbuf,
    send_p, send_f, recv_f, recv_p, recv_w, other, wide_w, wide_k,
    local_sem, halo_send, halo_recv, p_send, p_recv, w_send, w_recv, f_send, f_recv,
):
    groups = lax.axis_size("sec")
    tiles = lax.axis_size("tile")
    me = lax.axis_index("sec")
    tile = lax.axis_index("tile")
    rows = force_hbm.shape[2]
    layers = force_hbm.shape[1]
    depth = groups * layers
    above, below = lax.rem(tile + 1, tiles), lax.rem(tile + tiles - 1, tiles)

    barrier = pltpu.get_barrier_semaphore()

    @pl.loop(1, groups)
    def _(k):
        pl.semaphore_signal(
            barrier, inc=1, device_id={"sec": lax.rem(me + k, groups)}, device_id_type=pl.DeviceIdType.MESH
        )

    for neighbour in (above, below):
        pl.semaphore_signal(barrier, inc=1, device_id={"tile": neighbour}, device_id_type=pl.DeviceIdType.MESH)

    loads = [
        pltpu.make_async_copy(source, target, local_sem.at[i])
        for i, (source, target) in enumerate(
            (
                (dest_hbm, dest),
                (pos_hbm, pos),
                (conf_hbm, conf),
                (flow_hbm, flow),
                (stiff_hbm, sbuf.at[:, pl.ds(HALO, rows), :]),
                (force_hbm, fbuf.at[:, :, pl.ds(HALO, rows), :]),
                (cross_hbm, zbuf),
            )
        )
    ]
    for load in loads:
        load.start()
    for load in loads[:4]:
        load.wait()

    count = conf.shape[0]
    place = pos[...]
    slot = dest[...] * 8 + (place // 4) * 4 + (place % 2) * 2 + (place // 2) % 2
    hot = (lax.broadcasted_iota(jnp.int32, (count, count), 0) == slot).astype(jnp.float32).astype(jnp.bfloat16)
    confidence = conf[...]
    payload = jnp.concatenate(
        [confidence * flow[pl.ds(0, count, stride=2), :], confidence * flow[pl.ds(1, count, stride=2), :], confidence],
        axis=1,
    )
    high, middle, low = [jnp.dot(hot, part, preferred_element_type=jnp.float32) for part in split3(payload)]
    grid = high + middle + low
    pull = [grid[:, c * LANES : (c + 1) * LANES].reshape(groups, 8, LANES) for c in range(2)]
    front, back = pair_halves(*pull)
    send_p[:, 0] = front
    send_p[:, 1] = back
    send_p[:, 2] = grid[:, 2 * LANES :].reshape(groups, 8, LANES)

    recv_f[0] = jnp.zeros_like(recv_f[0])
    recv_f[depth + 1] = jnp.zeros_like(recv_f[0])
    other[0] = jnp.zeros_like(recv_f[0])
    other[depth + 1] = jnp.zeros_like(recv_f[0])
    recv_p[depth] = jnp.zeros_like(recv_f[0])
    wide_w[depth] = jnp.zeros_like(recv_f[0])

    loads[4].wait()
    loads[5].wait()
    pl.semaphore_wait(barrier, groups - 1 + 2)

    def halo_copy(index, buffer, source, target, neighbour):
        lead = (slice(None),) * (len(buffer.shape) - 2)
        return pltpu.make_async_remote_copy(
            src_ref=buffer.at[lead + (pl.ds(source, HALO), slice(None))],
            dst_ref=buffer.at[lead + (pl.ds(target, HALO), slice(None))],
            send_sem=halo_send.at[index],
            recv_sem=halo_recv.at[index],
            device_id={"tile": neighbour},
            device_id_type=pl.DeviceIdType.MESH,
        )

    halos = [
        halo_copy(0, fbuf, rows, 0, above),
        halo_copy(1, fbuf, HALO, rows + HALO, below),
        halo_copy(2, sbuf, rows, 0, above),
        halo_copy(3, sbuf, HALO, rows + HALO, below),
    ]
    for halo in halos:
        halo.start()

    def patch_copies(source, target, peer):
        return (
            pltpu.make_async_remote_copy(
                src_ref=send_p.at[target, pl.ds(0, 2)],
                dst_ref=recv_p.at[pl.ds(2 * source, 2)],
                send_sem=p_send.at[target],
                recv_sem=p_recv.at[source],
                device_id={"sec": peer},
                device_id_type=pl.DeviceIdType.MESH,
            ),
            pltpu.make_async_remote_copy(
                src_ref=send_p.at[target, 2],
                dst_ref=recv_w.at[source],
                send_sem=w_send.at[target],
                recv_sem=w_recv.at[source],
                device_id={"sec": peer},
                device_id_type=pl.DeviceIdType.MESH,
            ),
        )

    def field_copy(source, target, peer):
        return pltpu.make_async_remote_copy(
            src_ref=send_f.at[target],
            dst_ref=recv_f.at[pl.ds(1 + 2 * source, 2)],
            send_sem=f_send.at[target],
            recv_sem=f_recv.at[source],
            device_id={"sec": peer},
            device_id_type=pl.DeviceIdType.MESH,
        )

    def peer_at(k):
        return lax.rem(me + k, groups)

    @pl.loop(1, groups)
    def _(k):
        peer = peer_at(k)
        for copy in patch_copies(me, peer, peer):
            copy.start()

    def pack(rb, layer, blocks):
        for k in range(4):
            pieces = [
                blocks[c][2 * k : 2 * k + 2, xb * LANES : (xb + 1) * LANES] for c in range(2) for xb in range(2)
            ]
            send_f[4 * rb + k, layer] = jnp.concatenate(pieces, axis=0)

    for layer in range(layers):
        vbuf[:, layer] = plane_steps(
            fbuf[:, layer, pl.ds(HALO, rows), :], sbuf[layer, pl.ds(HALO, rows), :][None]
        )

        @pl.loop(1, rows // 8 - 1)
        def _(rb):
            at = pl.ds(pl.multiple_of(rb * 8, 8), 8)
            pack(rb, layer, [vbuf[c, layer, at, :] for c in range(2)])

    @pl.loop(1, groups)
    def _(k):
        peer = peer_at(k)

        @pl.when((peer >= 4) & (peer < groups - 4))
        def _():
            field_copy(me, peer, peer).start()

    for halo in halos:
        halo.wait_recv()
    for side, base in ((0, 0), (1, rows - HALO)):
        outside = (tile == 0) if side == 0 else (tile == tiles - 1)
        for layer in range(layers):
            force = fbuf[:, layer, pl.ds(base, 3 * HALO), :]
            stiff = sbuf[layer, pl.ds(base, 3 * HALO), :][None]
            row = lax.broadcasted_iota(jnp.int32, force.shape, 1)
            edge = (row < HALO) if side == 0 else (row >= 2 * HALO)
            empty = edge & outside
            force = jnp.where(empty, 0.0, force)
            stiff = jnp.where(empty[:1], 0.0, stiff)
            field = plane_steps(force, stiff)
            pack(0 if side == 0 else rows // 8 - 1, layer, [field[c, HALO : 2 * HALO] for c in range(2)])

    @pl.loop(1, groups)
    def _(k):
        peer = peer_at(k)

        @pl.when((peer < 4) | (peer >= groups - 4))
        def _():
            field_copy(me, peer, peer).start()

    recv_f[pl.ds(1 + 2 * me, 2)] = send_f[me]
    recv_p[pl.ds(2 * me, 2)] = send_p[me, pl.ds(0, 2)]
    recv_w[me] = send_p[me, 2]
    loads[6].wait()

    def both(halves):
        lower = lax.broadcasted_iota(jnp.int32, halves.shape, 1) < 4
        turned = pltpu.roll(halves, 4, 1)
        return jnp.where(lower, halves, turned), jnp.where(lower, turned, halves)

    @pl.loop(0, groups)
    def _(s):
        even, odd = both(zbuf[pl.ds(s, 1)])
        wide_k[pl.ds(2 * s, 1)] = even
        wide_k[pl.ds(2 * s + 1, 1)] = odd

    @pl.loop(1, groups)
    def _(k):
        peer = peer_at(k)
        for copy in patch_copies(peer, peer, me):
            copy.wait_recv()

    @pl.loop(0, groups)
    def _(s):
        even, odd = both(recv_w[pl.ds(s, 1)])
        wide_w[pl.ds(2 * s, 1)] = even
        wide_w[pl.ds(2 * s + 1, 1)] = odd

    @pl.loop(1, groups)
    def _(k):
        peer = peer_at(k)
        field_copy(peer, peer, me).wait_recv()

    chunk = 8
    for step in range(ZSTEPS):
        source, target = (recv_f, other) if step % 2 == 0 else (other, recv_f)

        @pl.loop(0, depth // chunk)
        def _(i):
            z = pl.multiple_of(i * chunk, chunk)
            d = source[pl.ds(z, chunk + 2)]
            slope = d[1:] - d[:-1]
            stretch = recv_p[pl.ds(z, chunk + 1)] - wide_w[pl.ds(z, chunk + 1)] * slope
            bend = wide_k[pl.ds(z, chunk)] * (slope[1:] - slope[:-1])
            target[pl.ds(z + 1, chunk)] = d[1:-1] + STEP_CROSS * (bend + (stretch[:-1] - stretch[1:]))

    final = recv_f if ZSTEPS % 2 == 0 else other

    @pl.loop(0, groups)
    def _(s):
        even, odd = pair_halves(final[pl.ds(1 + 2 * s, 1)], final[pl.ds(2 + 2 * s, 1)])
        out_ref[0, pl.ds(s, 1)] = even
        out_ref[1, pl.ds(s, 1)] = odd

    for halo in halos:
        halo.wait_send()

    @pl.loop(1, groups)
    def _(k):
        peer = peer_at(k)
        for copy in patch_copies(me, peer, peer) + (field_copy(me, peer, peer),):
            copy.wait_send()


def per_device(
    in_plane_force, stiffness, stiffness_z, patch_dest, patch_pos, patch_flow, patch_conf
):
    groups = lax.axis_size("sec")
    _, layers, rows, columns = in_plane_force.shape
    inner_rows = rows // groups
    width = patch_flow.shape[-1]
    blocks = columns // width
    count = patch_pos.shape[2]
    depth = layers * groups
    cross = (
        stiffness_z.reshape(depth, inner_rows, blocks, width)
        .transpose(0, 2, 1, 3)
        .reshape(groups, layers * blocks * inner_rows, width)
    )
    f32, dma = jnp.float32, pltpu.SemaphoreType.DMA
    vmem = pltpu.VMEM
    out = pl.pallas_call(
        body,
        out_shape=jax.ShapeDtypeStruct((2, groups, 8, width), f32),
        in_specs=[pl.BlockSpec(memory_space=pl.ANY)] * 7,
        out_specs=pl.BlockSpec(memory_space=pltpu.VMEM),
        scratch_shapes=[
            vmem((2, layers, rows + 2 * HALO, columns), f32),
            vmem((layers, rows + 2 * HALO, columns), f32),
            vmem((groups, 8, width), f32),
            vmem((1, count), jnp.int32),
            vmem((1, count), jnp.int32),
            vmem((2 * count, width), f32),
            vmem((count, width), f32),
            vmem((2, layers, rows, columns), f32),
            vmem((groups, 3, 8, width), f32),
            vmem((groups, 2, 8, width), f32),
            vmem((depth + 2, 8, width), f32),
            vmem((depth + 1, 8, width), f32),
            vmem((groups, 8, width), f32),
            vmem((depth + 2, 8, width), f32),
            vmem((depth + 1, 8, width), f32),
            vmem((depth, 8, width), f32),
            dma((7,)),
            dma((4,)),
            dma((4,)),
            dma((groups,)),
            dma((groups,)),
            dma((groups,)),
            dma((groups,)),
            dma((groups,)),
            dma((groups,)),
        ],
        compiler_params=pltpu.CompilerParams(collective_id=0, has_side_effects=True),
        name="relax",
    )(
        in_plane_force,
        stiffness,
        cross,
        patch_dest.reshape(1, count),
        patch_pos.reshape(1, count),
        patch_flow.reshape(2 * count, width),
        patch_conf.reshape(count, width),
    )
    return (
        out.reshape(2, depth, blocks, inner_rows, width)
        .transpose(0, 1, 3, 2, 4)
        .reshape(2, depth, inner_rows, columns)
    )


def solution(mesh):
    placed = (
        P(None, "sec", "tile", None),
        P("sec", "tile", None),
        P(None, ("tile", "sec"), None),
        P("sec", "tile", None, None),
        P("sec", "tile", None),
        P("sec", "tile", None, None, None),
        P("sec", "tile", None, None),
    )
    return jax.shard_map(
        per_device,
        mesh=mesh,
        in_specs=placed,
        out_specs=P(None, None, ("tile", "sec"), None),
        check_vma=False,
    )
```

time: 213 us -> 44 us (0.21)
  the two profiles are of different devices: /device:TPU:25 before, /device:TPU:1 now
where the time goes in v1:
time: 44 us; the launch traced here: 43.8 us
  Pallas kernels  42.1 us (96%)
  local copies, waits for them, and re-layouts  1.67 us (4%)
    pallas_call x1, Pallas kernels, per_device(): pl.pallas_call(body, out_shape=jax.ShapeDtypeStruct((2, groups, 8, width)...  42.1 us
    unnamed x1, local copies, waits for them, and re-layouts  1.67 us

profile of v1, /device:TPU:1, one launch (start us, length us, event | category | flops | bytes accessed | tf_op | source)
XLA Modules:
  0.0 43.8 jit_solution(14942559088483178906)
XLA Ops:
  0.0 42.1 %relax.1 = f32[2,32,8,128]{3,2,1,0:T(8,128)} custom-call(f32[2,2,64,256]{3,2,1,0:T(8,128)} %force_hbm.1, f32[2,64,256]{2,1,0:T(8,128)} %stiff_hbm.1, f32[32,8,128]{2,1,0:T(8,128)} %bitcast.16, s32[1,256]{1,0:T(1,128)} %bitcast.18, s32[1,256]{1,0:T(1,128)} %bitcast.19, f32[512,128]{1,0:T(8,128)} %bitcast.15, f32[256,128]{1,0:T(8,128)} %bitcast.17), custom_call_target="tpu_custom_call" | custom-call | tf_op jit(solution)/shard_map/relax/pallas_call | solution.py:306
  42.1 1.7 %copy.11 = f32[2,64,2,256]{3,2,1,0:T(2,128)} copy(f32[2,64,2,256]{3,2,1,0:T(2,128)} %bitcast.14) | data formatting | bytes 524288

commit v2 on v1

v2 whole, which is shorter than its diff:
```python
import functools

import jax
import jax.numpy as jnp
from jax import lax
from jax.experimental import pallas as pl
from jax.experimental.pallas import tpu as pltpu
from jax.sharding import PartitionSpec as P

ISTEPS = 8
ZSTEPS = 8
STEP_PLANE = 0.12
STEP_CROSS = 0.15
LANES = 128
HALO = 8
RUN = 4
CHUNK = 16


def plane_steps(force, stiff):
    column = lax.broadcasted_iota(jnp.int32, force.shape, 2)
    first, last = column == 0, column == force.shape[2] - 1
    field = STEP_PLANE * force
    for _ in range(1, ISTEPS):
        up = pltpu.roll(field, 1, 1)
        down = pltpu.roll(field, field.shape[1] - 1, 1)
        left = jnp.where(first, 0.0, pltpu.roll(field, 1, 2))
        right = jnp.where(last, 0.0, pltpu.roll(field, field.shape[2] - 1, 2))
        laplace = (up + down) + (left + right) - 4.0 * field
        field = field + STEP_PLANE * (stiff * laplace + force)
    return field


def split3(value):
    high = value.astype(jnp.bfloat16)
    rest = value - high.astype(jnp.float32)
    middle = rest.astype(jnp.bfloat16)
    low = (rest - middle.astype(jnp.float32)).astype(jnp.bfloat16)
    return high, middle, low


def pair_halves(a, b):
    lower = lax.broadcasted_iota(jnp.int32, a.shape, 1) < 4
    return jnp.where(lower, a, pltpu.roll(b, 4, 1)), jnp.where(lower, pltpu.roll(a, 4, 1), b)


def body(
    force_hbm, stiff_hbm, cross_hbm, dest_hbm, pos_hbm, flow_hbm, conf_hbm, out_ref,
    fbuf, sbuf, zbuf, dest, pos, flow, conf, vbuf,
    send_p, send_f, recv_f, recv_p, other, near, far, bend,
    local_sem, halo_send, halo_recv, p_send, p_recv, f_send, f_recv, ready,
):
    groups = lax.axis_size("sec")
    tiles = lax.axis_size("tile")
    me = lax.axis_index("sec")
    tile = lax.axis_index("tile")
    rows = force_hbm.shape[2]
    layers = force_hbm.shape[1]
    depth = groups * layers
    mesh = pl.DeviceIdType.MESH

    has_side = (tile > 0, tile < tiles - 1)
    neighbour = (lax.rem(tile + tiles - 1, tiles), lax.rem(tile + 1, tiles))
    greets = (lax.rem(tile, RUN) == 0, lax.rem(tile, RUN) != RUN - 1)

    barrier = pltpu.get_barrier_semaphore()

    def peer_at(k):
        return lax.rem(me + k, groups)

    @pl.loop(1, groups)
    def _(k):
        pl.semaphore_signal(barrier, inc=1, device_id={"sec": peer_at(k)}, device_id_type=mesh)

    for side in range(2):

        @pl.when(has_side[side] & greets[side])
        def _():
            pl.semaphore_signal(barrier, inc=1, device_id={"tile": neighbour[side]}, device_id_type=mesh)

    loads = [
        pltpu.make_async_copy(source, target, local_sem.at[i])
        for i, (source, target) in enumerate(
            (
                (dest_hbm, dest),
                (pos_hbm, pos),
                (conf_hbm, conf),
                (flow_hbm, flow),
                (stiff_hbm, sbuf.at[:, pl.ds(HALO, rows), :]),
                (force_hbm, fbuf.at[:, :, pl.ds(HALO, rows), :]),
                (cross_hbm, zbuf),
            )
        )
    ]
    for load in loads:
        load.start()
    for load in loads[:4]:
        load.wait()

    count = conf.shape[0]
    place = pos[...]
    slot = dest[...] * 8 + (place // 4) * 4 + (place % 2) * 2 + (place // 2) % 2
    hot = (lax.broadcasted_iota(jnp.int32, (count, count), 0) == slot).astype(jnp.float32).astype(jnp.bfloat16)
    confidence = conf[...]
    payload = jnp.concatenate(
        [confidence * flow[pl.ds(0, count, stride=2), :], confidence * flow[pl.ds(1, count, stride=2), :], confidence],
        axis=1,
    )
    high, middle, low = [jnp.dot(hot, part, preferred_element_type=jnp.float32) for part in split3(payload)]
    grid = high + middle + low
    pull = [grid[:, c * LANES : (c + 1) * LANES].reshape(groups, 8, LANES) for c in range(2)]
    front, back = pair_halves(*pull)
    send_p[:, 0] = front
    send_p[:, 1] = back
    send_p[:, 2] = grid[:, 2 * LANES :].reshape(groups, 8, LANES)

    blank = jnp.zeros((8, LANES), jnp.float32)
    for buffer in (recv_f, other):
        buffer[0] = blank
        buffer[depth + 1] = blank

    loads[4].wait()
    loads[5].wait()
    waits = groups - 1
    for side in range(2):
        waits = waits + (has_side[side] & jnp.logical_not(greets[side])).astype(jnp.int32)
    pl.semaphore_wait(barrier, waits)

    def halo_copy(index, buffer, side):
        lead = (slice(None),) * (len(buffer.shape) - 2)
        source, target = ((HALO, rows + HALO), (rows, 0))[side]
        return pltpu.make_async_remote_copy(
            src_ref=buffer.at[lead + (pl.ds(source, HALO), slice(None))],
            dst_ref=buffer.at[lead + (pl.ds(target, HALO), slice(None))],
            send_sem=halo_send.at[index, side],
            recv_sem=halo_recv.at[index, 1 - side],
            device_id={"tile": neighbour[side]},
            device_id_type=mesh,
        )

    def halo_copies(side):
        return halo_copy(0, fbuf, side), halo_copy(1, sbuf, side)

    def halo_arrivals(side):
        return halo_copies(1 - side)

    for side in range(2):

        @pl.when(has_side[side] & jnp.logical_not(greets[side]))
        def _():
            pl.semaphore_signal(ready.at[1 - side], inc=1, device_id={"tile": neighbour[side]}, device_id_type=mesh)
            for copy in halo_copies(side):
                copy.start()

    def patch_copy(peer):
        return pltpu.make_async_remote_copy(
            src_ref=send_p.at[peer],
            dst_ref=recv_p.at[me],
            send_sem=p_send,
            recv_sem=p_recv,
            device_id={"sec": peer},
            device_id_type=mesh,
        )

    def field_copy(peer):
        return pltpu.make_async_remote_copy(
            src_ref=send_f.at[peer],
            dst_ref=recv_f.at[pl.ds(1 + 2 * me, 2)],
            send_sem=f_send,
            recv_sem=f_recv,
            device_id={"sec": peer},
            device_id_type=mesh,
        )

    @pl.loop(1, groups)
    def _(k):
        patch_copy(peer_at(k)).start()

    def pack(rb, layer, blocks):
        for k in range(4):
            pieces = [
                blocks[c][2 * k : 2 * k + 2, xb * LANES : (xb + 1) * LANES] for c in range(2) for xb in range(2)
            ]
            send_f[4 * rb + k, layer] = jnp.concatenate(pieces, axis=0)

    for layer in range(layers):
        vbuf[:, layer] = plane_steps(
            fbuf[:, layer, pl.ds(HALO, rows), :], sbuf[layer, pl.ds(HALO, rows), :][None]
        )

        @pl.loop(1, rows // 8 - 1)
        def _(rb):
            at = pl.ds(pl.multiple_of(rb * 8, 8), 8)
            pack(rb, layer, [vbuf[c, layer, at, :] for c in range(2)])

    @pl.loop(1, groups)
    def _(k):
        peer = peer_at(k)

        @pl.when((peer >= 4) & (peer < groups - 4))
        def _():
            field_copy(peer).start()

    for side in (1, 0):

        @pl.when(has_side[side] & greets[side])
        def _():
            pl.semaphore_wait(ready.at[side], 1)
            for copy in halo_copies(side):
                copy.start()

    def both(halves):
        lower = lax.broadcasted_iota(jnp.int32, halves.shape, 1) < 4
        turned = pltpu.roll(halves, 4, 1)
        return jnp.where(lower, halves, turned), jnp.where(lower, turned, halves)

    loads[6].wait()
    recv_p[me] = send_p[me]

    for side, base in ((1, rows - HALO), (0, 0)):

        @pl.when(has_side[side])
        def _():
            for copy in halo_arrivals(side):
                copy.wait_recv()

        for layer in range(layers):
            force = fbuf[:, layer, pl.ds(base, 3 * HALO), :]
            stiff = sbuf[layer, pl.ds(base, 3 * HALO), :][None]
            row = lax.broadcasted_iota(jnp.int32, force.shape, 1)
            edge = (row < HALO) if side == 0 else (row >= 2 * HALO)
            empty = edge & jnp.logical_not(has_side[side])
            force = jnp.where(empty, 0.0, force)
            stiff = jnp.where(empty[:1], 0.0, stiff)
            field = plane_steps(force, stiff)
            pack(0 if side == 0 else rows // 8 - 1, layer, [field[c, HALO : 2 * HALO] for c in range(2)])

        @pl.loop(0, 4)
        def _(k):
            peer = k if side == 0 else groups - 4 + k

            @pl.when(peer != me)
            def _():
                field_copy(peer).start()

    recv_f[pl.ds(1 + 2 * me, 2)] = send_f[me]

    pltpu.make_async_copy(recv_p.at[pl.ds(1, groups - 1)], recv_p.at[pl.ds(1, groups - 1)], p_recv).wait()

    @pl.loop(0, groups - 1)
    def _(s):
        one, two = pl.ds(2 * s, 1), pl.ds(2 * s + 1, 1)
        k_even, k_odd = both(zbuf[pl.ds(s, 1)])
        w_even, w_odd = both(recv_p[pl.ds(s, 1), 2])
        w_next, _ = both(recv_p[pl.ds(s + 1, 1), 2])
        p_even, p_odd, p_next = recv_p[pl.ds(s, 1), 0], recv_p[pl.ds(s, 1), 1], recv_p[pl.ds(s + 1, 1), 0]
        near[one] = STEP_CROSS * (k_even + w_even)
        near[two] = STEP_CROSS * (k_odd + w_odd)
        far[one] = STEP_CROSS * (k_even + w_odd)
        far[two] = STEP_CROSS * (k_odd + w_next)
        bend[one] = STEP_CROSS * (p_even - p_odd)
        bend[two] = STEP_CROSS * (p_odd - p_next)

    k_even, k_odd = both(zbuf[pl.ds(groups - 1, 1)])
    w_even, w_odd = both(recv_p[pl.ds(groups - 1, 1), 2])
    p_even, p_odd = recv_p[pl.ds(groups - 1, 1), 0], recv_p[pl.ds(groups - 1, 1), 1]
    near[pl.ds(depth - 2, 1)] = STEP_CROSS * (k_even + w_even)
    near[pl.ds(depth - 1, 1)] = STEP_CROSS * (k_odd + w_odd)
    far[pl.ds(depth - 2, 1)] = STEP_CROSS * (k_even + w_odd)
    far[pl.ds(depth - 1, 1)] = STEP_CROSS * k_odd
    bend[pl.ds(depth - 2, 1)] = STEP_CROSS * (p_even - p_odd)
    bend[pl.ds(depth - 1, 1)] = STEP_CROSS * p_odd

    pltpu.make_async_copy(recv_f.at[pl.ds(1, depth - 2)], recv_f.at[pl.ds(1, depth - 2)], f_recv).wait()

    for step in range(ZSTEPS):
        source, target = (recv_f, other) if step % 2 == 0 else (other, recv_f)

        @pl.loop(0, depth // CHUNK)
        def _(i):
            z = pl.multiple_of(i * CHUNK, CHUNK)
            d = source[pl.ds(z, CHUNK + 2)]
            slope = d[1:] - d[:-1]
            at = pl.ds(z, CHUNK)
            d = d[1:-1] + ((far[at] * slope[1:] - near[at] * slope[:-1]) + bend[at])
            if step < ZSTEPS - 1:
                target[pl.ds(z + 1, CHUNK)] = d
            else:
                d = d.reshape(CHUNK // 2, 2, 8, LANES)
                even, odd = pair_halves(d[:, 0], d[:, 1])
                half = pl.ds(pl.multiple_of(i * (CHUNK // 2), CHUNK // 2), CHUNK // 2)
                out_ref[0, half] = even
                out_ref[1, half] = odd

    for side in range(2):

        @pl.when(has_side[side])
        def _():
            for copy in halo_copies(side):
                copy.wait_send()

    pltpu.make_async_copy(send_p.at[pl.ds(1, groups - 1)], send_p.at[pl.ds(1, groups - 1)], p_send).wait()
    pltpu.make_async_copy(send_f.at[pl.ds(1, groups - 1)], send_f.at[pl.ds(1, groups - 1)], f_send).wait()


def per_device(
    in_plane_force, stiffness, stiffness_z, patch_dest, patch_pos, patch_flow, patch_conf
):
    groups = lax.axis_size("sec")
    _, layers, rows, columns = in_plane_force.shape
    inner_rows = rows // groups
    width = patch_flow.shape[-1]
    blocks = columns // width
    count = patch_pos.shape[2]
    depth = layers * groups
    cross = (
        stiffness_z.reshape(depth, inner_rows, blocks, width)
        .transpose(0, 2, 1, 3)
        .reshape(groups, layers * blocks * inner_rows, width)
    )
    f32, dma = jnp.float32, pltpu.SemaphoreType.DMA
    vmem = pltpu.VMEM
    out = pl.pallas_call(
        body,
        out_shape=pltpu.VMEM((2, groups, 8, width), f32),
        in_specs=[pl.BlockSpec(memory_space=pl.ANY)] * 7,
        out_specs=pl.BlockSpec(memory_space=pltpu.VMEM),
        scratch_shapes=[
            vmem((2, layers, rows + 2 * HALO, columns), f32),
            vmem((layers, rows + 2 * HALO, columns), f32),
            vmem((groups, 8, width), f32),
            vmem((1, count), jnp.int32),
            vmem((1, count), jnp.int32),
            vmem((2 * count, width), f32),
            vmem((count, width), f32),
            vmem((2, layers, rows, columns), f32),
            vmem((groups, 3, 8, width), f32),
            vmem((groups, 2, 8, width), f32),
            vmem((depth + 2, 8, width), f32),
            vmem((groups, 3, 8, width), f32),
            vmem((depth + 2, 8, width), f32),
            vmem((depth, 8, width), f32),
            vmem((depth, 8, width), f32),
            vmem((depth, 8, width), f32),
            dma((7,)),
            dma((2, 2)),
            dma((2, 2)),
            dma(()),
            dma(()),
            dma(()),
            dma(()),
            pltpu.SemaphoreType.REGULAR((2,)),
        ],
        compiler_params=pltpu.CompilerParams(collective_id=0, has_side_effects=True),
        name="relax",
    )(
        in_plane_force,
        stiffness,
        cross,
        patch_dest.reshape(1, count),
        patch_pos.reshape(1, count),
        patch_flow.reshape(2 * count, width),
        patch_conf.reshape(count, width),
    )
    return (
        out.reshape(2, depth, blocks, inner_rows, width)
        .transpose(0, 1, 3, 2, 4)
        .reshape(2, depth, inner_rows, columns)
    )


def solution(mesh):
    placed = (
        P(None, "sec", "tile", None),
        P("sec", "tile", None),
        P(None, ("tile", "sec"), None),
        P("sec", "tile", None, None),
        P("sec", "tile", None),
        P("sec", "tile", None, None, None),
        P("sec", "tile", None, None),
    )
    return jax.shard_map(
        per_device,
        mesh=mesh,
        in_specs=placed,
        out_specs=P(None, None, ("tile", "sec"), None),
        check_vma=False,
    )
```

time: 44 us -> 33.3 us (0.76)
  the two profiles are of different devices: /device:TPU:1 before, /device:TPU:385 now
where the time goes in v2:
time: 33.3 us; the launch traced here: 33.1 us
  Pallas kernels  32.4 us (97%)
  local copies, waits for them, and re-layouts  0.71 us (2%)
    pallas_call x1, Pallas kernels, per_device(): pl.pallas_call(body, out_shape=pltpu.VMEM((2, groups, 8, width), f32), in...  32.4 us
    unnamed x1, local copies, waits for them, and re-layouts  0.71 us

profile of v2, /device:TPU:385, one launch (start us, length us, event | category | flops | bytes accessed | tf_op | source)
XLA Modules:
  0.0 33.1 jit_solution(11998961066300261467)
XLA Ops:
  0.0 32.4 %relax.1 = f32[2,32,8,128]{3,2,1,0:T(8,128)S(1)} custom-call(f32[2,2,64,256]{3,2,1,0:T(8,128)} %force_hbm.1, f32[2,64,256]{2,1,0:T(8,128)} %stiff_hbm.1, f32[32,8,128]{2,1,0:T(8,128)} %bitcast.16, s32[1,256]{1,0:T(1,128)} %bitcast.18, s32[1,256]{1,0:T(1,128)} %bitcast.19, f32[512,128]{1,0:T(8,128)} %bitcast.15, f32[256,128]{1,0:T(8,128)} %bitcast.17), custom_call_target="tpu_custom_call" | custom-call | tf_op jit(solution)/shard_map/relax/pallas_call | solution.py:323
  32.4 0.7 %copy.11 = f32[2,64,2,256]{3,2,1,0:T(2,128)} copy(f32[2,64,2,256]{3,2,1,0:T(2,128)S(1)} %bitcast.14) | data formatting | bytes 524288

commit v3 on v2

--- a/solution.py
+++ b/solution.py
@@ -14,7 +14,7 @@
 LANES = 128
 HALO = 8
 RUN = 4
-CHUNK = 16
+CHUNK = 32
 
 
 def plane_steps(force, stiff):
@@ -48,7 +48,7 @@
     force_hbm, stiff_hbm, cross_hbm, dest_hbm, pos_hbm, flow_hbm, conf_hbm, out_ref,
     fbuf, sbuf, zbuf, dest, pos, flow, conf, vbuf,
     send_p, send_f, recv_f, recv_p, other, near, far, bend,
-    local_sem, halo_send, halo_recv, p_send, p_recv, f_send, f_recv, ready,
+    local_sem, halo_send, halo_recv, p_send, p_recv, f_send, f_recv, ready, met,
 ):
     groups = lax.axis_size("sec")
     tiles = lax.axis_size("tile")
@@ -65,18 +65,42 @@
 
     barrier = pltpu.get_barrier_semaphore()
 
+    core = lax.rem(me, 2)
+    partner = me + 1 - 2 * core
+
+    half = groups // 2
+    split = lax.rem(tile, RUN) < RUN // 2
+
+    direct = lax.rem(tile, RUN) == RUN // 2
+
+    def in_first(peer):
+        return split & (peer > 0) & (peer < half)
+
     def peer_at(k):
-        return lax.rem(me + k, groups)
-
-    @pl.loop(1, groups)
+        away = lax.rem(me + jnp.where(core == 0, k, groups - k), groups)
+        level = jnp.where(split, k // 8, groups // 8 - 1 - k // 8)
+        return jnp.where(split | direct, level * 8 + lax.rem(me + k, 8), away)
+
+    first = in_first(me)
+
+    @pl.loop(0, half)
     def _(k):
-        pl.semaphore_signal(barrier, inc=1, device_id={"sec": peer_at(k)}, device_id_type=mesh)
+        collector = 2 * lax.rem(me // 2 + k, half) + 1 - first.astype(jnp.int32)
+
+        @pl.when(collector != me)
+        def _():
+            pl.semaphore_signal(barrier, inc=1, device_id={"sec": collector}, device_id_type=mesh)
+
+    @pl.when((core == 1) & jnp.logical_not(first))
+    def _():
+        pl.semaphore_signal(barrier, inc=1, device_id={"sec": partner}, device_id_type=mesh)
 
     for side in range(2):
 
         @pl.when(has_side[side] & greets[side])
         def _():
-            pl.semaphore_signal(barrier, inc=1, device_id={"tile": neighbour[side]}, device_id_type=mesh)
+            target = {"sec": me - core, "tile": neighbour[side]}
+            pl.semaphore_signal(barrier, inc=1, device_id=target, device_id_type=mesh)
 
     loads = [
         pltpu.make_async_copy(source, target, local_sem.at[i])
@@ -92,8 +116,50 @@
             )
         )
     ]
-    for load in loads:
+    def halo_copy(index, buffer, side):
+        lead = (slice(None),) * (len(buffer.shape) - 2)
+        reach = ISTEPS - 1 - index
+        source, target = ((HALO, rows + HALO), (rows + HALO - reach, HALO - reach))[side]
+        return pltpu.make_async_remote_copy(
+            src_ref=buffer.at[lead + (pl.ds(source, reach), slice(None))],
+            dst_ref=buffer.at[lead + (pl.ds(target, reach), slice(None))],
+            send_sem=halo_send.at[index, side],
+            recv_sem=halo_recv.at[index, 1 - side],
+            device_id={"tile": neighbour[side]},
+            device_id_type=mesh,
+        )
+
+    def halo_copies(side):
+        return halo_copy(0, fbuf, side), halo_copy(1, sbuf, side)
+
+    def meet():
+        @pl.when(core == 0)
+        def _():
+            members = half - 1 - first.astype(jnp.int32)
+            waits = jnp.where(split, members, 0) + (partner >= half).astype(jnp.int32)
+            waits = jnp.where(split, waits, 1)
+            for side in range(2):
+                waits = waits + 2 * (has_side[side] & jnp.logical_not(greets[side])).astype(jnp.int32)
+            pl.semaphore_wait(barrier, waits)
+            pl.semaphore_signal(met, inc=1, device_id={"sec": partner}, device_id_type=mesh)
+
+        @pl.when(core == 1)
+        def _():
+            pl.semaphore_wait(met, 1)
+
+        for side in range(2):
+
+            @pl.when(has_side[side] & jnp.logical_not(greets[side]))
+            def _():
+                pl.semaphore_signal(ready.at[1 - side], inc=1, device_id={"tile": neighbour[side]}, device_id_type=mesh)
+                for copy in halo_copies(side):
+                    copy.start()
+
+    for load in loads[4:6] + loads[:4] + loads[6:]:
         load.start()
+    loads[4].wait()
+    loads[5].wait()
+    pl.when(jnp.logical_not(split))(meet)
     for load in loads[:4]:
         load.wait()
 
@@ -119,38 +185,7 @@
         buffer[0] = blank
         buffer[depth + 1] = blank
 
-    loads[4].wait()
-    loads[5].wait()
-    waits = groups - 1
-    for side in range(2):
-        waits = waits + (has_side[side] & jnp.logical_not(greets[side])).astype(jnp.int32)
-    pl.semaphore_wait(barrier, waits)
-
-    def halo_copy(index, buffer, side):
-        lead = (slice(None),) * (len(buffer.shape) - 2)
-        source, target = ((HALO, rows + HALO), (rows, 0))[side]
-        return pltpu.make_async_remote_copy(
-            src_ref=buffer.at[lead + (pl.ds(source, HALO), slice(None))],
-            dst_ref=buffer.at[lead + (pl.ds(target, HALO), slice(None))],
-            send_sem=halo_send.at[index, side],
-            recv_sem=halo_recv.at[index, 1 - side],
-            device_id={"tile": neighbour[side]},
-            device_id_type=mesh,
-        )
-
-    def halo_copies(side):
-        return halo_copy(0, fbuf, side), halo_copy(1, sbuf, side)
-
-    def halo_arrivals(side):
-        return halo_copies(1 - side)
-
-    for side in range(2):
-
-        @pl.when(has_side[side] & jnp.logical_not(greets[side]))
-        def _():
-            pl.semaphore_signal(ready.at[1 - side], inc=1, device_id={"tile": neighbour[side]}, device_id_type=mesh)
-            for copy in halo_copies(side):
-                copy.start()
+    pl.when(split)(meet)
 
     def patch_copy(peer):
         return pltpu.make_async_remote_copy(
@@ -172,9 +207,24 @@
             device_id_type=mesh,
         )
 
-    @pl.loop(1, groups)
-    def _(k):
-        patch_copy(peer_at(k)).start()
+    def answer(when):
+        for side in (1, 0):
+
+            @pl.when(when & has_side[side] & greets[side])
+            def _():
+                pl.semaphore_wait(ready.at[side], 1)
+                for copy in halo_copies(side):
+                    copy.start()
+
+    @pl.when(split)
+    def _():
+        @pl.loop(0, half)
+        def _(k):
+            peer = peer_at(k)
+
+            @pl.when(in_first(peer) & (peer != me))
+            def _():
+                patch_copy(peer).start()
 
     def pack(rb, layer, blocks):
         for k in range(4):
@@ -193,21 +243,41 @@
             at = pl.ds(pl.multiple_of(rb * 8, 8), 8)
             pack(rb, layer, [vbuf[c, layer, at, :] for c in range(2)])
 
-    @pl.loop(1, groups)
-    def _(k):
-        peer = peer_at(k)
-
-        @pl.when((peer >= 4) & (peer < groups - 4))
-        def _():
-            field_copy(peer).start()
-
-    for side in (1, 0):
-
-        @pl.when(has_side[side] & greets[side])
-        def _():
-            pl.semaphore_wait(ready.at[side], 1)
-            for copy in halo_copies(side):
-                copy.start()
+    @pl.when(core == 1)
+    def _():
+        others = jnp.where(split, half + 1, groups)
+        pl.semaphore_wait(barrier, others - (jnp.logical_not(first)).astype(jnp.int32))
+        pl.semaphore_signal(met, inc=1, device_id={"sec": partner}, device_id_type=mesh)
+
+    @pl.when(core == 0)
+    def _():
+        pl.semaphore_wait(met, 1)
+
+    answer(direct)
+
+    def send_patches(low, high):
+        @pl.loop(low, high)
+        def _(k):
+            peer = peer_at(k)
+
+            @pl.when(jnp.logical_not(in_first(peer)) & (peer != me))
+            def _():
+                patch_copy(peer).start()
+
+    send_patches(0, groups)
+    answer(jnp.logical_not(direct))
+
+    def send_inner(low, high, late):
+        @pl.loop(low, high)
+        def _(k):
+            peer = peer_at(k)
+            held = split & (lax.rem(peer, 8) < 4)
+
+            @pl.when((peer >= 4) & (peer < groups - 4) & (peer != me) & (held == late))
+            def _():
+                field_copy(peer).start()
+
+    send_inner(0, half, False)
 
     def both(halves):
         lower = lax.broadcasted_iota(jnp.int32, halves.shape, 1) < 4
@@ -217,31 +287,43 @@
     loads[6].wait()
     recv_p[me] = send_p[me]
 
-    for side, base in ((1, rows - HALO), (0, 0)):
-
-        @pl.when(has_side[side])
-        def _():
-            for copy in halo_arrivals(side):
-                copy.wait_recv()
+    lead = lax.rem(tile, RUN) == 0
+
+    @pl.loop(0, 2)
+    def _(turn):
+        side = jnp.where(lead, turn, 1 - turn)
+        inside = jnp.where(side == 0, tile > 0, tile < tiles - 1)
+        base = pl.multiple_of(side * (rows - HALO), HALO)
+
+        @pl.when(inside)
+        def _():
+            for index, buffer in enumerate((fbuf, sbuf)):
+                reach = ISTEPS - 1 - index
+                block = buffer.at[(slice(None),) * (len(buffer.shape) - 2) + (pl.ds(HALO, reach), slice(None))]
+                pltpu.make_async_copy(block, block, halo_recv.at[index, side]).wait()
 
         for layer in range(layers):
             force = fbuf[:, layer, pl.ds(base, 3 * HALO), :]
             stiff = sbuf[layer, pl.ds(base, 3 * HALO), :][None]
             row = lax.broadcasted_iota(jnp.int32, force.shape, 1)
-            edge = (row < HALO) if side == 0 else (row >= 2 * HALO)
-            empty = edge & jnp.logical_not(has_side[side])
+            edge = jnp.where(side == 0, row, 3 * HALO - 1 - row) < HALO
+            empty = edge & jnp.logical_not(inside)
             force = jnp.where(empty, 0.0, force)
             stiff = jnp.where(empty[:1], 0.0, stiff)
             field = plane_steps(force, stiff)
-            pack(0 if side == 0 else rows // 8 - 1, layer, [field[c, HALO : 2 * HALO] for c in range(2)])
+            pack(side * (rows // 8 - 1), layer, [field[c, HALO : 2 * HALO] for c in range(2)])
 
         @pl.loop(0, 4)
         def _(k):
-            peer = k if side == 0 else groups - 4 + k
+            peer = k + side * (groups - 4)
 
             @pl.when(peer != me)
             def _():
                 field_copy(peer).start()
+
+    send_inner(0, half, True)
+    send_inner(half, groups, False)
+    send_inner(half, groups, True)
 
     recv_f[pl.ds(1 + 2 * me, 2)] = send_f[me]
 
@@ -350,6 +432,7 @@
             dma(()),
             dma(()),
             pltpu.SemaphoreType.REGULAR((2,)),
+            pltpu.SemaphoreType.REGULAR,
         ],
         compiler_params=pltpu.CompilerParams(collective_id=0, has_side_effects=True),
         name="relax",

time: 33.3 us -> 29.9 us (0.90)
  the two profiles are of different devices: /device:TPU:385 before, /device:TPU:345 now
where the time goes in v3:
time: 29.9 us; the launch traced here: 29.8 us
  Pallas kernels  29.1 us (97%)
  local copies, waits for them, and re-layouts  0.71 us (2%)
    pallas_call x1, Pallas kernels, per_device(): pl.pallas_call(body, out_shape=pltpu.VMEM((2, groups, 8, width), f32), in...  29.1 us
    unnamed x1, local copies, waits for them, and re-layouts  0.71 us

profile of v3, /device:TPU:345, one launch (start us, length us, event | category | flops | bytes accessed | tf_op | source)
XLA Modules:
  0.0 29.8 jit_solution(10664599052608633942)
XLA Ops:
  0.0 29.1 %relax.1 = f32[2,32,8,128]{3,2,1,0:T(8,128)S(1)} custom-call(f32[2,2,64,256]{3,2,1,0:T(8,128)} %force_hbm.1, f32[2,64,256]{2,1,0:T(8,128)} %stiff_hbm.1, f32[32,8,128]{2,1,0:T(8,128)} %bitcast.16, s32[1,256]{1,0:T(1,128)} %bitcast.18, s32[1,256]{1,0:T(1,128)} %bitcast.19, f32[512,128]{1,0:T(8,128)} %bitcast.15, f32[256,128]{1,0:T(8,128)} %bitcast.17), custom_call_target="tpu_custom_call" | custom-call | tf_op jit(solution)/shard_map/relax/pallas_call | solution.py:405
  29.1 0.7 %copy.11 = f32[2,64,2,256]{3,2,1,0:T(2,128)} copy(f32[2,64,2,256]{3,2,1,0:T(2,128)S(1)} %bitcast.14) | data formatting | bytes 524288

commit v4 on v3

--- a/solution.py
+++ b/solution.py
@@ -15,17 +15,20 @@
 HALO = 8
 RUN = 4
 CHUNK = 32
+DEFER = 24
 
 
 def plane_steps(force, stiff):
-    column = lax.broadcasted_iota(jnp.int32, force.shape, 2)
-    first, last = column == 0, column == force.shape[2] - 1
+    y, x = force.ndim - 2, force.ndim - 1
+    rows, columns = force.shape[y:]
+    column = lax.broadcasted_iota(jnp.int32, force.shape, x)
+    first, last = column == 0, column == columns - 1
     field = STEP_PLANE * force
     for _ in range(1, ISTEPS):
-        up = pltpu.roll(field, 1, 1)
-        down = pltpu.roll(field, field.shape[1] - 1, 1)
-        left = jnp.where(first, 0.0, pltpu.roll(field, 1, 2))
-        right = jnp.where(last, 0.0, pltpu.roll(field, field.shape[2] - 1, 2))
+        up = pltpu.roll(field, 1, y)
+        down = pltpu.roll(field, rows - 1, y)
+        left = jnp.where(first, 0.0, pltpu.roll(field, 1, x))
+        right = jnp.where(last, 0.0, pltpu.roll(field, columns - 1, x))
         laplace = (up + down) + (left + right) - 4.0 * field
         field = field + STEP_PLANE * (stiff * laplace + force)
     return field
@@ -83,6 +86,17 @@
 
     first = in_first(me)
 
+    @pl.when((core == 1) & jnp.logical_not(first))
+    def _():
+        pl.semaphore_signal(barrier, inc=1, device_id={"sec": partner}, device_id_type=mesh)
+
+    for side in range(2):
+
+        @pl.when(has_side[side] & greets[side])
+        def _():
+            target = {"sec": me - core, "tile": neighbour[side]}
+            pl.semaphore_signal(barrier, inc=1, device_id=target, device_id_type=mesh)
+
     @pl.loop(0, half)
     def _(k):
         collector = 2 * lax.rem(me // 2 + k, half) + 1 - first.astype(jnp.int32)
@@ -90,17 +104,6 @@
         @pl.when(collector != me)
         def _():
             pl.semaphore_signal(barrier, inc=1, device_id={"sec": collector}, device_id_type=mesh)
-
-    @pl.when((core == 1) & jnp.logical_not(first))
-    def _():
-        pl.semaphore_signal(barrier, inc=1, device_id={"sec": partner}, device_id_type=mesh)
-
-    for side in range(2):
-
-        @pl.when(has_side[side] & greets[side])
-        def _():
-            target = {"sec": me - core, "tile": neighbour[side]}
-            pl.semaphore_signal(barrier, inc=1, device_id=target, device_id_type=mesh)
 
     loads = [
         pltpu.make_async_copy(source, target, local_sem.at[i])
@@ -116,12 +119,12 @@
             )
         )
     ]
-    def halo_copy(index, buffer, side):
+    def halo_copy(index, values, buffer, side):
         lead = (slice(None),) * (len(buffer.shape) - 2)
         reach = ISTEPS - 1 - index
-        source, target = ((HALO, rows + HALO), (rows + HALO - reach, HALO - reach))[side]
+        source, target = ((0, rows + HALO), (rows - reach, HALO - reach))[side]
         return pltpu.make_async_remote_copy(
-            src_ref=buffer.at[lead + (pl.ds(source, reach), slice(None))],
+            src_ref=values.at[lead + (pl.ds(source, reach), slice(None))],
             dst_ref=buffer.at[lead + (pl.ds(target, reach), slice(None))],
             send_sem=halo_send.at[index, side],
             recv_sem=halo_recv.at[index, 1 - side],
@@ -130,7 +133,7 @@
         )
 
     def halo_copies(side):
-        return halo_copy(0, fbuf, side), halo_copy(1, sbuf, side)
+        return halo_copy(0, force_hbm, fbuf, side), halo_copy(1, stiff_hbm, sbuf, side)
 
     def meet():
         @pl.when(core == 0)
@@ -155,12 +158,10 @@
                 for copy in halo_copies(side):
                     copy.start()
 
-    for load in loads[4:6] + loads[:4] + loads[6:]:
+    for load in loads:
         load.start()
-    loads[4].wait()
-    loads[5].wait()
     pl.when(jnp.logical_not(split))(meet)
-    for load in loads[:4]:
+    for load in loads[:6]:
         load.wait()
 
     count = conf.shape[0]
@@ -264,20 +265,21 @@
             def _():
                 patch_copy(peer).start()
 
-    send_patches(0, groups)
+    send_patches(0, DEFER)
     answer(jnp.logical_not(direct))
-
-    def send_inner(low, high, late):
-        @pl.loop(low, high)
+    send_patches(DEFER, groups)
+
+    def send_inner(late):
+        @pl.loop(0, groups)
         def _(k):
             peer = peer_at(k)
-            held = split & (lax.rem(peer, 8) < 4)
+            held = (lax.rem(peer, 8) < 4) == (peer < half)
 
             @pl.when((peer >= 4) & (peer < groups - 4) & (peer != me) & (held == late))
             def _():
                 field_copy(peer).start()
 
-    send_inner(0, half, False)
+    send_inner(False)
 
     def both(halves):
         lower = lax.broadcasted_iota(jnp.int32, halves.shape, 1) < 4
@@ -287,7 +289,7 @@
     loads[6].wait()
     recv_p[me] = send_p[me]
 
-    lead = lax.rem(tile, RUN) == 0
+    lead = (lax.rem(tile, RUN) == 0) | (lax.rem(tile, RUN) == RUN - 1)
 
     @pl.loop(0, 2)
     def _(turn):
@@ -302,16 +304,16 @@
                 block = buffer.at[(slice(None),) * (len(buffer.shape) - 2) + (pl.ds(HALO, reach), slice(None))]
                 pltpu.make_async_copy(block, block, halo_recv.at[index, side]).wait()
 
+        force = fbuf[:, :, pl.ds(base, 3 * HALO), :]
+        stiff = sbuf[:, pl.ds(base, 3 * HALO), :][None]
+        row = lax.broadcasted_iota(jnp.int32, force.shape, 2)
+        edge = jnp.where(side == 0, row, 3 * HALO - 1 - row) < HALO
+        empty = edge & jnp.logical_not(inside)
+        force = jnp.where(empty, 0.0, force)
+        stiff = jnp.where(empty[:1], 0.0, stiff)
+        field = plane_steps(force, stiff)
         for layer in range(layers):
-            force = fbuf[:, layer, pl.ds(base, 3 * HALO), :]
-            stiff = sbuf[layer, pl.ds(base, 3 * HALO), :][None]
-            row = lax.broadcasted_iota(jnp.int32, force.shape, 1)
-            edge = jnp.where(side == 0, row, 3 * HALO - 1 - row) < HALO
-            empty = edge & jnp.logical_not(inside)
-            force = jnp.where(empty, 0.0, force)
-            stiff = jnp.where(empty[:1], 0.0, stiff)
-            field = plane_steps(force, stiff)
-            pack(side * (rows // 8 - 1), layer, [field[c, HALO : 2 * HALO] for c in range(2)])
+            pack(side * (rows // 8 - 1), layer, [field[c, layer, HALO : 2 * HALO] for c in range(2)])
 
         @pl.loop(0, 4)
         def _(k):
@@ -321,9 +323,7 @@
             def _():
                 field_copy(peer).start()
 
-    send_inner(0, half, True)
-    send_inner(half, groups, False)
-    send_inner(half, groups, True)
+    send_inner(True)
 
     recv_f[pl.ds(1 + 2 * me, 2)] = send_f[me]
 

time: 29.9 us -> 29.3 us (0.980)
  the two profiles are of different devices: /device:TPU:345 before, /device:TPU:25 now
where the time goes in v4:
time: 29.3 us; the launch traced here: 28.9 us
  Pallas kernels  28.2 us (96%)
  local copies, waits for them, and re-layouts  0.71 us (2%)
    pallas_call x1, Pallas kernels, per_device(): pl.pallas_call(body, out_shape=pltpu.VMEM((2, groups, 8, width), f32), in...  28.2 us
    unnamed x1, local copies, waits for them, and re-layouts  0.71 us

profile of v4, /device:TPU:25, one launch (start us, length us, event | category | flops | bytes accessed | tf_op | source)
XLA Modules:
  0.0 28.9 jit_solution(17866998702977027166)
XLA Ops:
  0.0 28.2 %relax.1 = f32[2,32,8,128]{3,2,1,0:T(8,128)S(1)} custom-call(f32[2,2,64,256]{3,2,1,0:T(8,128)} %force_hbm.1, f32[2,64,256]{2,1,0:T(8,128)} %stiff_hbm.1, f32[32,8,128]{2,1,0:T(8,128)} %bitcast.16, s32[1,256]{1,0:T(1,128)} %bitcast.18, s32[1,256]{1,0:T(1,128)} %bitcast.19, f32[512,128]{1,0:T(8,128)} %bitcast.15, f32[256,128]{1,0:T(8,128)} %bitcast.17), custom_call_target="tpu_custom_call" | custom-call | tf_op jit(solution)/shard_map/relax/pallas_call | solution.py:405
  28.2 0.7 %copy.11 = f32[2,64,2,256]{3,2,1,0:T(2,128)} copy(f32[2,64,2,256]{3,2,1,0:T(2,128)S(1)} %bitcast.14) | data formatting | bytes 524288

commit v5 on v4

--- a/solution.py
+++ b/solution.py
@@ -19,19 +19,24 @@
 
 
 def plane_steps(force, stiff):
-    y, x = force.ndim - 2, force.ndim - 1
-    rows, columns = force.shape[y:]
-    column = lax.broadcasted_iota(jnp.int32, force.shape, x)
-    first, last = column == 0, column == columns - 1
-    field = STEP_PLANE * force
+    rows, columns = force.shape[1:]
+    drive, pace = STEP_PLANE * force, STEP_PLANE * stiff
+    keep = 1.0 - 4.0 * pace
+    blocks = [slice(at, at + LANES) for at in range(0, columns, LANES)]
+    drive, pace, keep = [[value[..., block] for block in blocks] for value in (drive, pace, keep)]
+    lane = lax.broadcasted_iota(jnp.int32, drive[0].shape, 2)
+    first, last = lane == 0, lane == LANES - 1
+    field = drive
     for _ in range(1, ISTEPS):
-        up = pltpu.roll(field, 1, y)
-        down = pltpu.roll(field, rows - 1, y)
-        left = jnp.where(first, 0.0, pltpu.roll(field, 1, x))
-        right = jnp.where(last, 0.0, pltpu.roll(field, columns - 1, x))
-        laplace = (up + down) + (left + right) - 4.0 * field
-        field = field + STEP_PLANE * (stiff * laplace + force)
-    return field
+        right = [pltpu.roll(value, LANES - 1, 2) for value in field] + [0.0]
+        left = [0.0] + [pltpu.roll(value, 1, 2) for value in field]
+        stepped = []
+        for i, value in enumerate(field):
+            beside = jnp.where(first, left[i], left[i + 1]) + jnp.where(last, right[i + 1], right[i])
+            around = beside + (pltpu.roll(value, 1, 1) + pltpu.roll(value, rows - 1, 1))
+            stepped.append(keep[i] * value + (pace[i] * around + drive[i]))
+        field = stepped
+    return jnp.concatenate(field, axis=2)
 
 
 def split3(value):
@@ -80,9 +85,8 @@
         return split & (peer > 0) & (peer < half)
 
     def peer_at(k):
-        away = lax.rem(me + jnp.where(core == 0, k, groups - k), groups)
-        level = jnp.where(split, k // 8, groups // 8 - 1 - k // 8)
-        return jnp.where(split | direct, level * 8 + lax.rem(me + k, 8), away)
+        level = jnp.where(direct, groups // 8 - 1 - k // 8, k // 8)
+        return level * 8 + lax.rem(me + k, 8)
 
     first = in_first(me)
 
@@ -96,14 +100,6 @@
         def _():
             target = {"sec": me - core, "tile": neighbour[side]}
             pl.semaphore_signal(barrier, inc=1, device_id=target, device_id_type=mesh)
-
-    @pl.loop(0, half)
-    def _(k):
-        collector = 2 * lax.rem(me // 2 + k, half) + 1 - first.astype(jnp.int32)
-
-        @pl.when(collector != me)
-        def _():
-            pl.semaphore_signal(barrier, inc=1, device_id={"sec": collector}, device_id_type=mesh)
 
     loads = [
         pltpu.make_async_copy(source, target, local_sem.at[i])
@@ -161,6 +157,15 @@
     for load in loads:
         load.start()
     pl.when(jnp.logical_not(split))(meet)
+
+    @pl.loop(0, half, unroll=True)
+    def _(k):
+        collector = 2 * lax.rem(me // 2 + k, half) + 1 - first.astype(jnp.int32)
+
+        @pl.when(collector != me)
+        def _():
+            pl.semaphore_signal(barrier, inc=1, device_id={"sec": collector}, device_id_type=mesh)
+
     for load in loads[:6]:
         load.wait()
 
@@ -269,17 +274,17 @@
     answer(jnp.logical_not(direct))
     send_patches(DEFER, groups)
 
-    def send_inner(late):
+    def send_inner():
         @pl.loop(0, groups)
         def _(k):
             peer = peer_at(k)
             held = (lax.rem(peer, 8) < 4) == (peer < half)
 
-            @pl.when((peer >= 4) & (peer < groups - 4) & (peer != me) & (held == late))
+            @pl.when((peer >= 4) & (peer < groups - 4) & (peer != me) & jnp.logical_not(held))
             def _():
                 field_copy(peer).start()
 
-    send_inner(False)
+    send_inner()
 
     def both(halves):
         lower = lax.broadcasted_iota(jnp.int32, halves.shape, 1) < 4
@@ -304,26 +309,27 @@
                 block = buffer.at[(slice(None),) * (len(buffer.shape) - 2) + (pl.ds(HALO, reach), slice(None))]
                 pltpu.make_async_copy(block, block, halo_recv.at[index, side]).wait()
 
-        force = fbuf[:, :, pl.ds(base, 3 * HALO), :]
-        stiff = sbuf[:, pl.ds(base, 3 * HALO), :][None]
-        row = lax.broadcasted_iota(jnp.int32, force.shape, 2)
-        edge = jnp.where(side == 0, row, 3 * HALO - 1 - row) < HALO
-        empty = edge & jnp.logical_not(inside)
-        force = jnp.where(empty, 0.0, force)
-        stiff = jnp.where(empty[:1], 0.0, stiff)
-        field = plane_steps(force, stiff)
         for layer in range(layers):
-            pack(side * (rows // 8 - 1), layer, [field[c, layer, HALO : 2 * HALO] for c in range(2)])
-
-        @pl.loop(0, 4)
-        def _(k):
-            peer = k + side * (groups - 4)
-
-            @pl.when(peer != me)
-            def _():
-                field_copy(peer).start()
-
-    send_inner(True)
+            force = fbuf[:, layer, pl.ds(base, 3 * HALO), :]
+            stiff = sbuf[layer, pl.ds(base, 3 * HALO), :][None]
+            row = lax.broadcasted_iota(jnp.int32, force.shape, 1)
+            edge = jnp.where(side == 0, row, 3 * HALO - 1 - row) < HALO
+            empty = edge & jnp.logical_not(inside)
+            force = jnp.where(empty, 0.0, force)
+            stiff = jnp.where(empty[:1], 0.0, stiff)
+            field = plane_steps(force, stiff)
+            pack(side * (rows // 8 - 1), layer, [field[c, HALO : 2 * HALO] for c in range(2)])
+
+        for block in (side * (groups - 4), 8 + side * (groups - 20)):
+
+            @pl.loop(0, 4)
+            def _(k):
+                peer = block + k
+
+                @pl.when(peer != me)
+                def _():
+                    field_copy(peer).start()
+
 
     recv_f[pl.ds(1 + 2 * me, 2)] = send_f[me]
 

time: 29.3 us -> 29.1 us (level)
  no operation moved by 1% of the time
where the time goes in v5:
time: 29.1 us; the launch traced here: 29 us
  Pallas kernels  28.2 us (97%)
  local copies, waits for them, and re-layouts  0.71 us (2%)
    pallas_call x1, Pallas kernels, per_device(): pl.pallas_call(body, out_shape=pltpu.VMEM((2, groups, 8, width), f32), in...  28.2 us
    unnamed x1, local copies, waits for them, and re-layouts  0.71 us

profile of v5, /device:TPU:25, one launch (start us, length us, event | category | flops | bytes accessed | tf_op | source)
XLA Modules:
  0.0 29.0 jit_solution(6897727171802878949)
XLA Ops:
  0.0 28.2 %relax.1 = f32[2,32,8,128]{3,2,1,0:T(8,128)S(1)} custom-call(f32[2,2,64,256]{3,2,1,0:T(8,128)} %force_hbm.1, f32[2,64,256]{2,1,0:T(8,128)} %stiff_hbm.1, f32[32,8,128]{2,1,0:T(8,128)} %bitcast.16, s32[1,256]{1,0:T(1,128)} %bitcast.18, s32[1,256]{1,0:T(1,128)} %bitcast.19, f32[512,128]{1,0:T(8,128)} %bitcast.15, f32[256,128]{1,0:T(8,128)} %bitcast.17), custom_call_target="tpu_custom_call" | custom-call | tf_op jit(solution)/shard_map/relax/pallas_call | solution.py:411
  28.2 0.7 %copy.11 = f32[2,64,2,256]{3,2,1,0:T(2,128)} copy(f32[2,64,2,256]{3,2,1,0:T(2,128)S(1)} %bitcast.14) | data formatting | bytes 524288

commit v6 on v5

--- a/solution.py
+++ b/solution.py
@@ -224,7 +224,7 @@
 
     @pl.when(split)
     def _():
-        @pl.loop(0, half)
+        @pl.loop(0, half, unroll=4)
         def _(k):
             peer = peer_at(k)
 
@@ -262,7 +262,7 @@
     answer(direct)
 
     def send_patches(low, high):
-        @pl.loop(low, high)
+        @pl.loop(low, high, unroll=4)
         def _(k):
             peer = peer_at(k)
 
@@ -275,7 +275,7 @@
     send_patches(DEFER, groups)
 
     def send_inner():
-        @pl.loop(0, groups)
+        @pl.loop(0, groups, unroll=4)
         def _(k):
             peer = peer_at(k)
             held = (lax.rem(peer, 8) < 4) == (peer < half)

time: 29.1 us -> 29.1 us (level)
  no operation moved by 1% of the time
where the time goes in v6:
time: 29.1 us; the launch traced here: 29 us
  Pallas kernels  28.2 us (97%)
  local copies, waits for them, and re-layouts  0.71 us (2%)
    pallas_call x1, Pallas kernels, per_device(): pl.pallas_call(body, out_shape=pltpu.VMEM((2, groups, 8, width), f32), in...  28.2 us
    unnamed x1, local copies, waits for them, and re-layouts  0.71 us

profile of v6, /device:TPU:25, one launch (start us, length us, event | category | flops | bytes accessed | tf_op | source)
XLA Modules:
  0.0 29.0 jit_solution(5689008601659067016)
XLA Ops:
  0.0 28.2 %relax.1 = f32[2,32,8,128]{3,2,1,0:T(8,128)S(1)} custom-call(f32[2,2,64,256]{3,2,1,0:T(8,128)} %force_hbm.1, f32[2,64,256]{2,1,0:T(8,128)} %stiff_hbm.1, f32[32,8,128]{2,1,0:T(8,128)} %bitcast.16, s32[1,256]{1,0:T(1,128)} %bitcast.18, s32[1,256]{1,0:T(1,128)} %bitcast.19, f32[512,128]{1,0:T(8,128)} %bitcast.15, f32[256,128]{1,0:T(8,128)} %bitcast.17), custom_call_target="tpu_custom_call" | custom-call | tf_op jit(solution)/shard_map/relax/pallas_call | solution.py:411
  28.2 0.7 %copy.11 = f32[2,64,2,256]{3,2,1,0:T(2,128)} copy(f32[2,64,2,256]{3,2,1,0:T(2,128)S(1)} %bitcast.14) | data formatting | bytes 524288

commit v7 on v6

--- a/solution.py
+++ b/solution.py
@@ -322,7 +322,7 @@
 
         for block in (side * (groups - 4), 8 + side * (groups - 20)):
 
-            @pl.loop(0, 4)
+            @pl.loop(0, 4, unroll=True)
             def _(k):
                 peer = block + k
 

time: 29.1 us -> 29 us (level)
  no operation moved by 1% of the time
where the time goes in v7:
time: 29 us; the launch traced here: 28.9 us
  Pallas kernels  28.2 us (97%)
  local copies, waits for them, and re-layouts  0.71 us (2%)
    pallas_call x1, Pallas kernels, per_device(): pl.pallas_call(body, out_shape=pltpu.VMEM((2, groups, 8, width), f32), in...  28.2 us
    unnamed x1, local copies, waits for them, and re-layouts  0.71 us

profile of v7, /device:TPU:25, one launch (start us, length us, event | category | flops | bytes accessed | tf_op | source)
XLA Modules:
  0.0 28.9 jit_solution(3564130503574905378)
XLA Ops:
  0.0 28.2 %relax.1 = f32[2,32,8,128]{3,2,1,0:T(8,128)S(1)} custom-call(f32[2,2,64,256]{3,2,1,0:T(8,128)} %force_hbm.1, f32[2,64,256]{2,1,0:T(8,128)} %stiff_hbm.1, f32[32,8,128]{2,1,0:T(8,128)} %bitcast.16, s32[1,256]{1,0:T(1,128)} %bitcast.18, s32[1,256]{1,0:T(1,128)} %bitcast.19, f32[512,128]{1,0:T(8,128)} %bitcast.15, f32[256,128]{1,0:T(8,128)} %bitcast.17), custom_call_target="tpu_custom_call" | custom-call | tf_op jit(solution)/shard_map/relax/pallas_call | solution.py:411
  28.2 0.7 %copy.11 = f32[2,64,2,256]{3,2,1,0:T(2,128)} copy(f32[2,64,2,256]{3,2,1,0:T(2,128)S(1)} %bitcast.14) | data formatting | bytes 524288
